TPU v7x, 32 devices: a whole 2x2x4 slice. The times are simulated.
32 devices in a mesh: grp: 2 (over y), seq: 4 (over z), head: 4 (over x, core).
Axes of the slice: x: 2, y: 2, z: 4, core: 2. Of those that a mesh axis runs over, the one named last changes fastest.
Arguments:
- queries: bfloat16 [5120, 8192], P(('grp', 'seq'), 'head'), parts along dimension 0, may hold values from -30 to 30, as said below
- keys: bfloat16 [5120, 8192], P(('grp', 'seq'), 'head'), parts along dimension 0, may hold values from -6 to 6
- values: bfloat16 [5120, 8192], P(('grp', 'seq'), 'head'), parts along dimension 0, may hold values from -24 to 24, as said below
- gain: bfloat16 [8192], P('head'), may hold values from 0.25 to 1.75
Outputs:
- output: bfloat16 [5120, 8192], P(('grp', 'seq'), 'head'), parts along dimension 0
There are 2 independent parts, one for each index of `grp`. A program takes and returns all parts, laid end to end along the dimension named above; an argument that names none is the same for every part. Nothing has to cross between parts.
Inputs may be any that keep to these rules, and one draw needn't show every extreme that they name: `queries`: query rows of various sizes. `values`: value features and rows of various sizes.
All inputs are finite; a program needn't handle non-finite values.
Results may differ from a plain program's by a relative error of at most 0.0051.
Values sent between devices are 32-bit elements; how exact they have to be, the bound alone decides.
No kernel may reach another device: no remote copies, remote signals or barrier semaphores. Data moves between devices by JAX's collectives and lax.ppermute only.
A program may use at most 64 MiB of HBM per device.

v0:
```python
import jax
import jax.numpy as jnp
from jax import lax
from jax.sharding import PartitionSpec as P

HEADS = 64
HEAD_DIM = 128


def body(queries, keys, values, gain):
    tokens_here = queries.shape[0]
    heads_here = queries.shape[1] // HEAD_DIM
    queries_split = queries.reshape(tokens_here, heads_here, HEAD_DIM)
    keys_split = keys.reshape(tokens_here, heads_here, HEAD_DIM)
    values_split = values.reshape(tokens_here, heads_here, HEAD_DIM)
    local_state = jnp.einsum(
        "thd,the->hde", keys_split, values_split, preferred_element_type=jnp.float32
    )
    my_index = lax.axis_index("seq")
    piece = lax.all_gather(local_state[None], "seq", axis=0, tiled=True)
    owners = jnp.arange(piece.shape[0], dtype=jnp.int32)
    weights = (owners < my_index).astype(jnp.float32)
    prefix = jnp.sum(piece * weights[:, None, None, None], axis=0)
    positions = jnp.arange(tokens_here)
    causal = positions[:, None] >= positions[None, :]
    scores = jnp.einsum(
        "thd,shd->hts", queries_split, keys_split, preferred_element_type=jnp.float32
    )
    scores = jnp.where(causal[None], scores, jnp.float32(0.0)).astype(jnp.bfloat16)
    intra_term = jnp.einsum(
        "hts,she->the", scores, values_split, preferred_element_type=jnp.float32
    )
    prefix_low = prefix.astype(jnp.bfloat16)
    inter_term = jnp.einsum(
        "thd,hde->the", queries_split, prefix_low, preferred_element_type=jnp.float32
    )
    mixed = (intra_term + inter_term).reshape(tokens_here, heads_here * HEAD_DIM)
    partial_squares = jnp.sum(mixed * mixed, axis=1)
    total_squares = lax.psum(partial_squares, "head")
    factor = lax.rsqrt(total_squares / (HEADS * HEAD_DIM) + 1e-06)
    return (mixed * factor[:, None] * gain.astype(jnp.float32)[None, :]).astype(jnp.bfloat16)


def solution(mesh):
    placed = (
        P(("grp", "seq"), "head"),
        P(("grp", "seq"), "head"),
        P(("grp", "seq"), "head"),
        P("head"),
    )
    return jax.shard_map(
        body, mesh=mesh, in_specs=placed, out_specs=P(("grp", "seq"), "head"), check_vma=False
    )
```

profile of v0, /device:TPU:0, one launch (start us, length us, event | category | flops | bytes accessed | tf_op | source)
XLA Modules:
  0.0 132.1 jit_solution(14653907628350191327)
XLA Ops:
  6.5 0.0 copy-start
  6.5 0.0 all-gather.3.cloned.1.call-start
  6.5 4.5 %copy.17 = bf16[640,2048]{0,1:T(8,128)(2,1)} copy(bf16[640,2048]{1,0:T(8,128)(2,1)} %param.5) | data formatting | bytes 5242880 | tf_op jit(solution)/shard_map/reshape | solution.py:14
  11.1 0.0 copy-start.1
  11.1 4.4 %fusion.2 = f32[16,128,128]{2,1,0:T(8,128)} fusion(bf16[640,16,128]{0,2,1:T(8,128)(2,1)} %bitcast.43, bf16[640,2048]{1,0:T(8,128)(2,1)} %param.6), kind=kOutput, calls=%fused_computation.7 | convolution fusion | flops 335544320 | bytes 6291456 | tf_op jit(solution)/shard_map/thd,the->hde/dot_general | solution.py:16
  15.4 0.0 all-gather.3.cloned.1.call-update
  15.5 0.0 copy-done.1
  15.5 0.1 iota_compare_fusion
  15.6 0.0 copy-done
  15.6 10.9 %fusion = f32[16,640,128]{1,2,0:T(8,128)} fusion(bf16[640,16,128]{0,2,1:T(8,128)(2,1)} %bitcast.44, pred[640,640]{1,0:T(8,128)(4,1)S(1)} %iota_compare_fusion, bf16[640,2048]{1,0:T(8,128)(2,1)} %param.6, bf16[640,2048]{1,0:T(8,128)(2,1)S(1)} %copy-done), kind=kOutput, calls=%fused_computation.5 | convolution fusion | flops 3368550400 | bytes 13516800 | tf_op jit(solution)/shard_map/hts,she->the/dot_general | solution.py:30
  26.5 72.6 %all-gather.3.cloned.1.call-done = f32[64,128,128]{2,1,0:T(8,128)} async-done(((f32[16,128,128]{2,1,0:T(8,128)}), f32[64,128,128]{2,1,0:T(8,128)}) %all-gather.3.cloned.1.call-update) | async-done | bytes 4194320 | tf_op jit(solution)/shard_map/all_gather | solution.py:20
  99.1 2.7 %multiply_reduce_fusion.1 = bf16[16,128,128]{2,1,0:T(8,128)(2,1)S(1)} fusion(f32[4,16,128,128]{3,2,1,0:T(8,128)} %bitcast.42, f32[4]{0:T(128)S(1)} %compare_convert_fusion), kind=kLoop, calls=%fused_computation.4 | loop fusion | flops 1835008 | bytes 4718608 | tf_op jit(solution)/shard_map/reduce_sum | solution.py:23
  101.8 6.0 %multiply_reduce_fusion = (f32[640]{0:T(1024)S(1)}, f32[640,16,128]{0,2,1:T(8,128)}) fusion(bf16[16,128,128]{2,1,0:T(8,128)(2,1)S(1)} %multiply_reduce_fusion.1, f32[16,640,128]{1,2,0:T(8,128)} %fusion, bf16[640,2048]{1,0:T(8,128)(2,1)S(1)} %copy-done), kind=kOutput, calls=%fused_computation.3 | convolution fusion | flops 339475840 | bytes 13634048 | tf_op jit(solution)/shard_map/thd,hde->the/dot_general | solution.py:34
  107.8 6.0 %copy.15 = f32[640,2048]{1,0:T(8,128)} copy(f32[640,2048]{0,1:T(8,128)} %bitcast.41) | data formatting | bytes 10485760 | tf_op jit(solution)/shard_map/reshape | solution.py:37
  113.9 6.9 %psum.7 = f32[640]{0:T(1024)S(1)} all-reduce(f32[640]{0:T(1024)S(1)} %get-tuple-element.5), channel_id=1, replica_groups=mesh['grp'=2,'seq'=4,'head'=4] {'head'}, use_global_device_ids=true, to_apply=%region_2.3 | all-reduce | flops 640 | bytes 5120 | tf_op jit(solution)/shard_map/psum | solution.py:39
  120.7 4.5 %multiply_convert_fusion = bf16[640,2048]{1,0:T(8,128)(2,1)} fusion(f32[640,2048]{1,0:T(8,128)} %copy.15, f32[2048]{0:T(1024)S(1)} %convert_element_type.22, f32[640]{0:T(1024)S(1)} %add_rsqrt_fusion), kind=kLoop, calls=%fused_computation.2 | loop fusion | flops 3932160 | bytes 7875072 | tf_op jit(solution)/shard_map/convert_element_type | solution.py:41
  (3 shorter events, 0.0 us)
Async XLA Ops:
  6.5 9.1 %copy-start = (bf16[640,2048]{1,0:T(8,128)(2,1)S(1)}, bf16[640,2048]{1,0:T(8,128)(2,1)}, u32[]{:S(2)}) copy-start(bf16[640,2048]{1,0:T(8,128)(2,1)} %param.4) | copy-start | bytes 7864324
  6.5 92.5 %all-gather.3.cloned.1.call-start = ((), (), s32[]{:S(2)}) async-start(), calls=%async_computation | async-start | bytes 5242880 | tf_op jit(solution)/shard_map/all_gather | solution.py:20
  11.1 4.4 %copy-start.1 = (bf16[2048]{0:T(1024)(128)(2,1)S(1)}, bf16[2048]{0:T(1024)(128)(2,1)}, u32[]{:S(2)}) copy-start(bf16[2048]{0:T(1024)(128)(2,1)} %param.7) | copy-start | bytes 12292
Sparse Core Ops, SparseCore 0:
  15.6 83.4 all-gather.2
where the time goes:
time: 132 us
  waiting for transfers between devices  72.6 us (55%)
  matrix products  21.3 us (16%)
  between operations  13.4 us (10%)
  local copies, waits for them, and re-layouts  10.6 us (8%)
  other arithmetic  7.33 us (6%)
  blocking collectives  6.86 us (5%)
    all_gather x1, waiting for transfers between devices, body(): piece = lax.all_gather(local_state[None], 'seq', axis=0, tiled=True)  72.6 us
    dot_general x1, matrix products, body(): jnp.einsum('hts,she->the', scores, values_split, preferred_element_type=j...  10.9 us
    psum x1, blocking collectives, body(): total_squares = lax.psum(partial_squares, 'head')  6.86 us
    reshape x1, local copies, waits for them, and re-layouts, body(): (intra_term + inter_term).reshape(tokens_here, heads_here * HEAD_DIM)  6.05 us
    dot_general x1, matrix products, body(): jnp.einsum('thd,hde->the', queries_split, prefix_low, preferred_element_t...  6.03 us
    reshape x1, local copies, waits for them, and re-layouts, body(): keys_split = keys.reshape(tokens_here, heads_here, HEAD_DIM)  4.52 us
    convert_element_type x1, other arithmetic, body(): (mixed * factor[:, None] * gain.astype(jnp.float32)[None, :]).astype(jnp....  4.47 us
    dot_general x1, matrix products, body(): jnp.einsum('thd,the->hde', keys_split, values_split, preferred_element_ty...  4.37 us
  transfers between devices with their start and end apart: 1, of which 1 were waited for; matrix products, arithmetic and copies ran while one was open for 8% of the time, Pallas kernels for 0%

commit v1 on v0

v1 whole, which is shorter than its diff:
```python
import functools

import jax
import jax.numpy as jnp
from jax import lax
from jax.experimental import pallas as pl
from jax.experimental.pallas import tpu as pltpu
from jax.sharding import PartitionSpec as P

HEAD_DIM = 128
CHUNK_HEADS = 2
LAG = 2
F32 = jnp.float32
BF16 = jnp.bfloat16
NT = ((1,), (1,))
NN = ((1,), (0,))
TN = ((0,), (0,))
VMEM = pl.BlockSpec(memory_space=pltpu.VMEM)
ANY = pl.BlockSpec(memory_space=pl.ANY)
LIMIT = 12 << 20


def dot(a, b, dims):
    return lax.dot_general(a, b, (dims, ((), ())), preferred_element_type=F32)


def head_columns(head):
    return slice(head * HEAD_DIM, (head + 1) * HEAD_DIM)


def first_state_body(k_ref, v_ref, out_ref):
    for h in range(CHUNK_HEADS):
        cols = head_columns(h)
        out_ref[h] = dot(k_ref[:, cols], v_ref[:, cols], TN)


def first_state(keys, values):
    tokens = keys.shape[0]
    block = pl.BlockSpec((tokens, CHUNK_HEADS * HEAD_DIM), lambda g: (0, 0))
    shape = (CHUNK_HEADS, HEAD_DIM, HEAD_DIM)
    return pl.pallas_call(
        first_state_body,
        grid=(1,),
        out_shape=jax.ShapeDtypeStruct(shape, F32),
        in_specs=[block, block],
        out_specs=pl.BlockSpec(shape, lambda g: (0, 0, 0)),
        compiler_params=pltpu.CompilerParams(vmem_limit_bytes=LIMIT),
        name="first_state",
    )(keys, values)


def merge_body(shards, has_received, *refs):
    *sources, out_ref = refs
    received = sources.pop(0) if has_received else None
    sources.pop()
    me = lax.axis_index("seq")
    value = sources[0][...]
    for source, shard in zip(sources[1:], shards[1:]):
        value = jnp.where(me >= shard, source[...], value)
    if has_received:
        value = value + received[...]
    out_ref[...] = value


def merge(shards, states, received, order):
    args = ([] if received is None else [received]) + states
    return pl.pallas_call(
        functools.partial(merge_body, shards, received is not None),
        out_shape=jax.ShapeDtypeStruct(states[0].shape, F32),
        in_specs=[VMEM] * len(args) + [ANY],
        out_specs=VMEM,
        compiler_params=pltpu.CompilerParams(vmem_limit_bytes=LIMIT),
        cost_estimate=pl.CostEstimate(flops=100000, bytes_accessed=10000, transcendentals=0),
        name="merge",
    )(*args, order)


def add_squares(mixed, squares):
    return mixed * mixed if squares is None else squares + mixed * mixed


def step_body(shards, chunks, intra, inter, final, has_squares, *refs):
    refs = list(refs)
    q_ref, k_ref, v_ref = refs[:3]
    refs = refs[3:]
    before = {}
    prefix = {}
    me = lax.axis_index("seq") if inter else None
    for c in inter:
        value = refs.pop(0)[...]
        for shard in range(2, shards):
            value = jnp.where(me >= shard, refs.pop(0)[...], value)
        prefix[c] = value.astype(BF16)
        for h in range(c * CHUNK_HEADS, (c + 1) * CHUNK_HEADS):
            before[h] = refs.pop(0)
    squares = refs.pop(0)[...] if has_squares else None
    refs = refs[2:]
    for c in chunks:
        state_ref = refs.pop(0)
        for h in range(CHUNK_HEADS):
            cols = head_columns(c * CHUNK_HEADS + h)
            state_ref[h] = dot(k_ref[:, cols], v_ref[:, cols], TN)
    for c in inter:
        for h in range(CHUNK_HEADS):
            head = c * CHUNK_HEADS + h
            mixed = before[head][...] + dot(q_ref[:, head_columns(head)], prefix[c][h], NN)
            refs.pop(0)[...] = mixed
            squares = add_squares(mixed, squares)
    if inter:
        if final:
            refs.pop(0)[...] = jnp.sum(squares.T, axis=0, keepdims=True)
        else:
            refs.pop(0)[...] = squares
    for head in intra:
        cols = head_columns(head)
        scores = dot(q_ref[:, cols], k_ref[:, cols], NT)
        row = lax.broadcasted_iota(jnp.int32, scores.shape, 0)
        column = lax.broadcasted_iota(jnp.int32, scores.shape, 1)
        scores = jnp.where(row >= column, scores, 0.0).astype(BF16)
        refs.pop(0)[...] = dot(scores, v_ref[:, cols], NN)


def step(shards, q, k, v, chunks, intra, inter, received, mixed, squares, order, final=False):
    tokens = q.shape[0]
    wide = jax.ShapeDtypeStruct((tokens, HEAD_DIM), F32)
    args, specs = [q, k, v], [VMEM] * 3
    for c in inter:
        came = [received[c + LAG * i] for i in range(shards - 1)]
        args += came
        args += [mixed[h] for h in range(c * CHUNK_HEADS, (c + 1) * CHUNK_HEADS)]
        specs += [VMEM] * (len(came) + CHUNK_HEADS)
    has_squares = bool(inter) and squares is not None
    if has_squares:
        args.append(squares)
        specs.append(VMEM)
    args += list(order)
    specs += [ANY] * 2
    out = [jax.ShapeDtypeStruct((CHUNK_HEADS, HEAD_DIM, HEAD_DIM), F32) for _ in chunks]
    out += [wide for _ in inter for _ in range(CHUNK_HEADS)]
    if inter:
        out.append(jax.ShapeDtypeStruct((1, tokens), F32) if final else wide)
    out += [wide for _ in intra]
    flops = 2 * tokens * HEAD_DIM * (
        HEAD_DIM * CHUNK_HEADS * (len(chunks) + len(inter)) + 2 * tokens * len(intra)
    )
    results = pl.pallas_call(
        functools.partial(step_body, shards, chunks, intra, inter, final, has_squares),
        out_shape=tuple(out),
        in_specs=specs,
        out_specs=tuple(VMEM for _ in out),
        compiler_params=pltpu.CompilerParams(vmem_limit_bytes=LIMIT),
        cost_estimate=pl.CostEstimate(flops=flops, bytes_accessed=100000, transcendentals=0),
        name="step",
    )(*args)
    results = list(results)
    states = {c: results.pop(0) for c in chunks}
    done = {}
    for c in inter:
        for h in range(c * CHUNK_HEADS, (c + 1) * CHUNK_HEADS):
            done[h] = results.pop(0)
    if inter:
        squares = results.pop(0)
    partial = {h: results.pop(0) for h in intra}
    return states, partial, done, squares


def finish_body(heads, width, *refs):
    mixed = refs[:heads]
    total_ref, gain_ref, out_ref, buf, sem = refs[heads:]
    tokens = buf.shape[0]
    factor = lax.rsqrt(total_ref[...] / width + 1e-06)
    factor = jnp.broadcast_to(factor, (HEAD_DIM, tokens)).T
    copies = []
    for c in range(heads // CHUNK_HEADS):
        for head in range(c * CHUNK_HEADS, (c + 1) * CHUNK_HEADS):
            cols = head_columns(head)
            buf[:, cols] = (mixed[head][...] * factor * gain_ref[:, cols].astype(F32)).astype(BF16)
        cols = slice(c * CHUNK_HEADS * HEAD_DIM, (c + 1) * CHUNK_HEADS * HEAD_DIM)
        copy = pltpu.make_async_copy(buf.at[:, cols], out_ref.at[:, cols], sem.at[c])
        copy.start()
        copies.append(copy)
    for copy in copies:
        copy.wait()


def finish(mixed, total, gain, width):
    heads = len(mixed)
    tokens = mixed[0].shape[0]
    return pl.pallas_call(
        functools.partial(finish_body, heads, float(width)),
        out_shape=jax.ShapeDtypeStruct((tokens, heads * HEAD_DIM), BF16),
        in_specs=[VMEM] * (heads + 2),
        out_specs=ANY,
        scratch_shapes=[
            pltpu.VMEM((tokens, heads * HEAD_DIM), BF16),
            pltpu.SemaphoreType.DMA((heads // CHUNK_HEADS,)),
        ],
        compiler_params=pltpu.CompilerParams(vmem_limit_bytes=LIMIT),
        name="finish",
    )(*mixed, total, gain)


def sum_over_heads(part, size):
    if size & (size - 1):
        return lax.psum(part, "head")
    reach = 1
    while reach < size:
        part = part + lax.ppermute(part, "head", [(i, i ^ reach) for i in range(size)])
        reach *= 2
    return part


def body(shards, head_shards, q, k, v, gain):
    heads = q.shape[1] // HEAD_DIM
    width = head_shards * q.shape[1]
    count = heads // CHUNK_HEADS
    last = count + LAG * (shards - 2)

    states = {0: first_state(k, v)}
    received = {}
    mixed = {}
    squares = None
    token = states[0]
    for s in range(last):
        senders = [i for i in range(shards - 1) if 0 <= s - LAG * i < count]
        if s == 0:
            mine = states[0]
        else:
            mine = merge(
                senders, [states[s - LAG * i] for i in senders], received.get(s - LAG), token
            )
        received[s] = lax.ppermute(mine, "seq", [(i, i + 1) for i in senders])

        chunks = list(range(1, count)) if s == 0 else []
        intra = [h for h in range(heads) if h * last // heads == s]
        inter = [c for c in range(count) if c + last - count + 2 == s]
        new_states, partial, done, squares = step(
            shards, q, k, v, chunks, intra, inter, received, mixed, squares, (mine, token)
        )
        states.update(new_states)
        mixed.update(partial)
        mixed.update(done)
        token = next(iter((*partial.values(), *done.values(), token)))
    for c in range(count - 2, count):
        _, _, done, squares = step(
            shards, q, k, v, [], [], [c], received, mixed, squares, (token, token), c == count - 1
        )
        mixed.update(done)
    total = sum_over_heads(squares, head_shards)
    return finish([mixed[h] for h in range(heads)], total, gain.reshape(1, -1), width)


def solution(mesh):
    placed = (
        P(("grp", "seq"), "head"),
        P(("grp", "seq"), "head"),
        P(("grp", "seq"), "head"),
        P("head"),
    )
    shape = dict(mesh.shape)
    return jax.shard_map(
        functools.partial(body, shape["seq"], shape["head"]),
        mesh=mesh,
        in_specs=placed,
        out_specs=P(("grp", "seq"), "head"),
        check_vma=False,
    )
```

time: 132 us -> 55.8 us (0.42)
  the two profiles are of different devices: /device:TPU:0 before, /device:TPU:24 now
where the time goes in v1:
time: 55.8 us; the launch traced here: 55.4 us
  waiting for transfers between devices  22.4 us (40%)
  starting transfers between devices  14.7 us (26%)
  Pallas kernels  14 us (25%)
  local copies, waits for them, and re-layouts  4.07 us (7%)
    ppermute x12, waiting for transfers between devices, body(): received[s] = lax.ppermute(mine, 'seq', [(i, i + 1) for i in senders])  19.1 us
    ppermute x12, starting transfers between devices, body(): received[s] = lax.ppermute(mine, 'seq', [(i, i + 1) for i in senders])  13.1 us
    pallas_call x14, Pallas kernels, step(): pl.pallas_call(functools.partial(step_body, shards, chunks, intra, inter,...  11.2 us
    unnamed x10, local copies, waits for them, and re-layouts  4.07 us
    ppermute x2, waiting for transfers between devices, sum_over_heads(): lax.ppermute(part, 'head', [(i, i ^ reach) for i in range(size)])  3.26 us
    pallas_call x1, Pallas kernels, finish(): pl.pallas_call(functools.partial(finish_body, heads, float(width)), out_s...  2.15 us
    ppermute x2, starting transfers between devices, sum_over_heads(): lax.ppermute(part, 'head', [(i, i ^ reach) for i in range(size)])  1.53 us
  transfers between devices with their start and end apart: 14, of which 10 were waited for; matrix products, arithmetic and copies ran while one was open for 0% of the time, Pallas kernels for 20%

profile of v1, /device:TPU:24, one launch (start us, length us, event | category | flops | bytes accessed | tf_op | source)
XLA Modules:
  0.0 55.4 jit_solution(3698354732124871375)
XLA Ops:
  0.0 0.0 copy-start
  0.0 1.7 %copy-done = bf16[640,2048]{1,0:T(8,128)(2,1)S(1)} copy-done((bf16[640,2048]{1,0:T(8,128)(2,1)S(1)}, bf16[640,2048]{1,0:T(8,128)(2,1)}, u32[]{:S(2)}) %copy-start) | copy-done | bytes 2621464
  1.7 0.0 copy-start.2
  1.7 1.7 %copy-done.2 = bf16[640,2048]{1,0:T(8,128)(2,1)S(1)} copy-done((bf16[640,2048]{1,0:T(8,128)(2,1)S(1)}, bf16[640,2048]{1,0:T(8,128)(2,1)}, u32[]{:S(2)}) %copy-start.2) | copy-done | bytes 2621464
  3.5 0.0 copy-start.3
  3.5 0.3 first_state.1.refs_3_.refs_4_.refs_2_
  3.8 0.0 copy-start.1
  3.8 0.8 %collective-permute-start = (f32[2,128,128]{2,1,0:T(8,128)S(1)}, f32[2,128,128]{2,1,0:T(8,128)S(1)}, u32[]{:S(2)}, u32[]{:S(2)}) collective-permute-start(f32[2,128,128]{2,1,0:T(8,128)S(1)} %first_state.1.refs_3_.refs_4_.refs_2_), channel_id=1, source_target_pairs={{0,4},{1,5},{2,6},{3,7},{16,20},{17,21},{18,22},{19,23}} | collective-permute-start | bytes 393224 | tf_op jit(solution)/shard_map/ppermute | solution.py:232
  4.6 0.6 %copy-done.3 = bf16[640,2048]{1,0:T(8,128)(2,1)S(1)} copy-done((bf16[640,2048]{1,0:T(8,128)(2,1)S(1)}, bf16[640,2048]{1,0:T(8,128)(2,1)}, u32[]{:S(2)}) %copy-start.3) | copy-done | bytes 2621464
  5.2 1.8 %step.14 = (f32[2,128,128]{2,1,0:T(8,128)S(1)}, f32[2,128,128]{2,1,0:T(8,128)S(1)}, f32[2,128,128]{2,1,0:T(8,128)S(1)}, f32[2,128,128]{2,1,0:T(8,128)S(1)}, f32[...) custom-call(bf16[640,2048]{1,0:T(8,128)(2,1)S(1)} %copy-done.3, ...), custom_call_target="tpu_custom_call" | custom-call | flops 713031680 | bytes 100000 | tf_op jit(solution)/shard_map/step/pallas_call | solution.py:146
  7.0 0.7 %collective-permute-start.2 = (f32[2,128,128]{2,1,0:T(8,128)S(1)}, f32[2,128,128]{2,1,0:T(8,128)S(1)}, u32[]{:S(2)}, u32[]{:S(2)}) collective-permute-start(f32[2,128,128]{2,1,0:T(8,128)S(1)} %merge.11.refs_3_), channel_id=1, source_target_pairs={{0,4},{1,5},{2,6},{3,7},{16,20},{17,21},{18,22},{19,23}} | collective-permute-start | bytes 393224 | tf_op jit(solution)/shard_map/ppermute | solution.py:232
  7.7 0.0 copy-done.1
  7.7 0.6 %step.15.refs_3_.refs_4_.refs_6_ = f32[640,128]{1,0:T(8,128)S(1)} custom-call(bf16[640,2048]{1,0:T(8,128)(2,1)S(1)} %copy-done.3, bf16[640,2048]{1,0:T(8,128)(2,1)S(1)} %copy-done.1, bf16[640,2048]{1,0:T(8,128)(2,1)S(1)} %copy-done.2, f32[2,128,128]{2,1,0:T(8,128)S(1)} %merge.11.refs_3_, f32[640,128]{1,0:T(8,128)S(1)} %get-tuple-element.50.refs_1_.refs_4_.refs_6_), custom_call_target="tpu_custom_call" | custom-call | flops 209715200 | bytes 100000 | tf_op jit(solution)/shard_map/step/pallas_call | solution.py:146
  8.4 0.0 collective-permute-done.refs_0_.refs_3_
  8.4 0.7 %collective-permute-start.1 = (f32[2,128,128]{2,1,0:T(8,128)S(1)}, f32[2,128,128]{2,1,0:T(8,128)S(1)}, u32[]{:S(2)}, u32[]{:S(2)}) collective-permute-start(f32[2,128,128]{2,1,0:T(8,128)S(1)} %merge.12.refs_3_), channel_id=1, source_target_pairs={{0,4},{4,8},{1,5},{5,9},{2,6},{6,10},{3,7},{7,11},{16,20},{20,24},... | collective-permute-start | bytes 393224 | tf_op jit(solution)/shard_map/ppermute | solution.py:232
  9.1 0.6 %step.16.refs_3_.refs_4_.refs_7_ = f32[640,128]{1,0:T(8,128)S(1)} custom-call(bf16[640,2048]{1,0:T(8,128)(2,1)S(1)} %copy-done.3, bf16[640,2048]{1,0:T(8,128)(2,1)S(1)} %copy-done.1, bf16[640,2048]{1,0:T(8,128)(2,1)S(1)} %copy-done.2, f32[2,128,128]{2,1,0:T(8,128)S(1)} %merge.12.refs_3_, f32[640,128]{1,0:T(8,128)S(1)} %step.15.refs_3_.refs_4_.refs_6_), custom_call_target="tpu_custom_call" | custom-call | flops 209715200 | bytes 100000 | tf_op jit(solution)/shard_map/step/pallas_call | solution.py:146
  9.7 0.0 collective-permute-done.2.refs_0_.refs_3_
  9.8 0.7 %collective-permute-start.4 = (f32[2,128,128]{2,1,0:T(8,128)S(1)}, f32[2,128,128]{2,1,0:T(8,128)S(1)}, u32[]{:S(2)}, u32[]{:S(2)}) collective-permute-start(f32[2,128,128]{2,1,0:T(8,128)S(1)} %merge.13.refs_3_), channel_id=1, source_target_pairs={{0,4},{4,8},{1,5},{5,9},{2,6},{6,10},{3,7},{7,11},{16,20},{20,24},... | collective-permute-start | bytes 393224 | tf_op jit(solution)/shard_map/ppermute | solution.py:232
  10.4 1.1 %step.17 = (f32[640,128]{1,0:T(8,128)S(1)}, f32[640,128]{1,0:T(8,128)S(1)}) custom-call(bf16[640,2048]{1,0:T(8,128)(2,1)S(1)} %copy-done.3, bf16[640,2048]{1,0:T(8,128)(2,1)S(1)} %copy-done.1, bf16[640,2048]{1,0:T(8,128)(2,1)S(1)} %copy-done.2, f32[2,128,128]{2,1,0:T(8,128)S(1)} %merge.13.refs_3_, f32[640,128]{1,0:T(8,128)S(1)} %step.16.refs_3_.refs_4_.refs_7_), custom_call_target="tpu_custom_call" | custom-call | flops 419430400 | bytes 100000 | tf_op jit(solution)/shard_map/step/pallas_call | solution.py:146
  11.5 0.0 collective-permute-done.1.refs_0_.refs_4_.refs_3_
  11.6 1.3 %collective-permute-start.3 = (f32[2,128,128]{2,1,0:T(8,128)S(1)}, f32[2,128,128]{2,1,0:T(8,128)S(1)}, u32[]{:S(2)}, u32[]{:S(2)}) collective-permute-start(f32[2,128,128]{2,1,0:T(8,128)S(1)} %merge.14.refs_3_), channel_id=1, source_target_pairs={{0,4},{4,8},{8,12},{1,5},{5,9},{9,13},{2,6},{6,10},{10,14},{3,7},{... | collective-permute-start | bytes 393224 | tf_op jit(solution)/shard_map/ppermute | solution.py:232
  12.9 0.6 %step.18.refs_4_.refs_6_ = f32[640,128]{1,0:T(8,128)S(1)} custom-call(bf16[640,2048]{1,0:T(8,128)(2,1)S(1)} %copy-done.3, bf16[640,2048]{1,0:T(8,128)(2,1)S(1)} %copy-done.1, bf16[640,2048]{1,0:T(8,128)(2,1)S(1)} %copy-done.2, f32[2,128,128]{2,1,0:T(8,128)S(1)} %merge.14.refs_3_, f32[640,128]{1,0:T(8,128)S(1)} %get-tuple-element.53.refs_4_.refs_6_), custom_call_target="tpu_custom_call" | custom-call | flops 209715200 | bytes 100000 | tf_op jit(solution)/shard_map/step/pallas_call | solution.py:146
  13.5 0.0 collective-permute-done.4.refs_0_.refs_4_.refs_3_
  13.6 1.3 %collective-permute-start.5 = (f32[2,128,128]{2,1,0:T(8,128)S(1)}, f32[2,128,128]{2,1,0:T(8,128)S(1)}, u32[]{:S(2)}, u32[]{:S(2)}) collective-permute-start(f32[2,128,128]{2,1,0:T(8,128)S(1)} %merge.15.refs_3_), channel_id=1, source_target_pairs={{0,4},{4,8},{8,12},{1,5},{5,9},{9,13},{2,6},{6,10},{10,14},{3,7},{... | collective-permute-start | bytes 393224 | tf_op jit(solution)/shard_map/ppermute | solution.py:232
  14.9 0.6 %step.19.refs_4_.refs_9_.refs_7_ = f32[640,128]{1,0:T(8,128)S(1)} custom-call(bf16[640,2048]{1,0:T(8,128)(2,1)S(1)} %copy-done.3, bf16[640,2048]{1,0:T(8,128)(2,1)S(1)} %copy-done.1, bf16[640,2048]{1,0:T(8,128)(2,1)S(1)} %copy-done.2, f32[2,128,128]{2,1,0:T(8,128)S(1)} %merge.15.refs_3_, f32[640,128]{1,0:T(8,128)S(1)} %step.18.refs_4_.refs_6_), custom_call_target="tpu_custom_call" | custom-call | flops 209715200 | bytes 100000 | tf_op jit(solution)/shard_map/step/pallas_call | solution.py:146
  15.5 7.3 %collective-permute-done.3.refs_0_.refs_5_.refs_4_.refs_3_ = f32[2,128,128]{2,1,0:T(8,128)S(1)} collective-permute-done((f32[2,128,128]{2,1,0:T(8,128)S(1)}, f32[2,128,128]{2,1,0:T(8,128)S(1)}, u32[]{:S(2)}, u32[]{:S(2)}) %collective-permute-start.3) | collective-permute-done | bytes 131104 | tf_op jit(solution)/shard_map/ppermute | solution.py:232
  22.9 1.3 %collective-permute-start.6 = (f32[2,128,128]{2,1,0:T(8,128)S(1)}, f32[2,128,128]{2,1,0:T(8,128)S(1)}, u32[]{:S(2)}, u32[]{:S(2)}) collective-permute-start(f32[2,128,128]{2,1,0:T(8,128)S(1)} %merge.16.refs_8_), channel_id=1, source_target_pairs={{0,4},{4,8},{8,12},{1,5},{5,9},{9,13},{2,6},{6,10},{10,14},{3,7},{... | collective-permute-start | bytes 393224 | tf_op jit(solution)/shard_map/ppermute | solution.py:232
  24.2 1.2 %step.20 = (f32[640,128]{1,0:T(8,128)S(1)}, f32[640,128]{1,0:T(8,128)S(1)}, f32[640,128]{1,0:T(8,128)S(1)}, f32[640,128]{1,0:T(8,128)S(1)}, f32[640,128]{1,0:T(8,128)S(1)}) custom-call(bf16[640,2048]{1,0:T(8,128)(2,1)S(1)} %copy-done.3, bf16[640,2048]{1,0:T(8,128)(2,1)S(1)} %copy-done.1, bf16[640,2048]{1,0:T(8,128)(2,1)S(1)} %copy-done.2, ...), custom_call_target="tpu_custom_call" | custom-call | flops 461373440 | bytes 100000 | tf_op jit(solution)/shard_map/step/pallas_call | solution.py:146
  25.3 0.6 %collective-permute-done.5.refs_0_.refs_5_.refs_4_.refs_3_ = f32[2,128,128]{2,1,0:T(8,128)S(1)} collective-permute-done((f32[2,128,128]{2,1,0:T(8,128)S(1)}, f32[2,128,128]{2,1,0:T(8,128)S(1)}, u32[]{:S(2)}, u32[]{:S(2)}) %collective-permute-start.5) | collective-permute-done | bytes 131104 | tf_op jit(solution)/shard_map/ppermute | solution.py:232
  26.0 1.3 %collective-permute-start.7 = (f32[2,128,128]{2,1,0:T(8,128)S(1)}, f32[2,128,128]{2,1,0:T(8,128)S(1)}, u32[]{:S(2)}, u32[]{:S(2)}) collective-permute-start(f32[2,128,128]{2,1,0:T(8,128)S(1)} %merge.17.refs_9_), channel_id=1, source_target_pairs={{0,4},{4,8},{8,12},{1,5},{5,9},{9,13},{2,6},{6,10},{10,14},{3,7},{... | collective-permute-start | bytes 393224 | tf_op jit(solution)/shard_map/ppermute | solution.py:232
  27.3 0.7 %step.21 = (f32[640,128]{1,0:T(8,128)S(1)}, f32[640,128]{1,0:T(8,128)S(1)}, f32[640,128]{1,0:T(8,128)S(1)}, f32[640,128]{1,0:T(8,128)S(1)}) custom-call(bf16[640,2048]{1,0:T(8,128)(2,1)S(1)} %copy-done.3, bf16[640,2048]{1,0:T(8,128)(2,1)S(1)} %copy-done.1, bf16[640,2048]{1,0:T(8,128)(2,1)S(1)} %copy-done.2, ...), custom_call_target="tpu_custom_call" | custom-call | flops 251658240 | bytes 100000 | tf_op jit(solution)/shard_map/step/pallas_call | solution.py:146
  28.0 3.0 %collective-permute-done.6.refs_0_.refs_5_.refs_4_.refs_3_ = f32[2,128,128]{2,1,0:T(8,128)S(1)} collective-permute-done((f32[2,128,128]{2,1,0:T(8,128)S(1)}, f32[2,128,128]{2,1,0:T(8,128)S(1)}, u32[]{:S(2)}, u32[]{:S(2)}) %collective-permute-start.6) | collective-permute-done | bytes 131104 | tf_op jit(solution)/shard_map/ppermute | solution.py:232
  31.1 1.3 %collective-permute-start.8 = (f32[2,128,128]{2,1,0:T(8,128)S(1)}, f32[2,128,128]{2,1,0:T(8,128)S(1)}, u32[]{:S(2)}, u32[]{:S(2)}) collective-permute-start(f32[2,128,128]{2,1,0:T(8,128)S(1)} %merge.18.refs_9_), channel_id=1, source_target_pairs={{4,8},{8,12},{5,9},{9,13},{6,10},{10,14},{7,11},{11,15},{20,24},{2... | collective-permute-start | bytes 393224 | tf_op jit(solution)/shard_map/ppermute | solution.py:232
  32.4 0.7 %step.22 = (f32[640,128]{1,0:T(8,128)S(1)}, f32[640,128]{1,0:T(8,128)S(1)}, f32[640,128]{1,0:T(8,128)S(1)}, f32[640,128]{1,0:T(8,128)S(1)}) custom-call(bf16[640,2048]{1,0:T(8,128)(2,1)S(1)} %copy-done.3, bf16[640,2048]{1,0:T(8,128)(2,1)S(1)} %copy-done.1, bf16[640,2048]{1,0:T(8,128)(2,1)S(1)} %copy-done.2, ...), custom_call_target="tpu_custom_call" | custom-call | flops 251658240 | bytes 100000 | tf_op jit(solution)/shard_map/step/pallas_call | solution.py:146
  33.1 1.1 %collective-permute-done.7.refs_0_.refs_5_.refs_4_.refs_3_ = f32[2,128,128]{2,1,0:T(8,128)S(1)} collective-permute-done((f32[2,128,128]{2,1,0:T(8,128)S(1)}, f32[2,128,128]{2,1,0:T(8,128)S(1)}, u32[]{:S(2)}, u32[]{:S(2)}) %collective-permute-start.7) | collective-permute-done | bytes 131104 | tf_op jit(solution)/shard_map/ppermute | solution.py:232
  34.2 1.3 %collective-permute-start.9 = (f32[2,128,128]{2,1,0:T(8,128)S(1)}, f32[2,128,128]{2,1,0:T(8,128)S(1)}, u32[]{:S(2)}, u32[]{:S(2)}) collective-permute-start(f32[2,128,128]{2,1,0:T(8,128)S(1)} %merge.19.refs_9_), channel_id=1, source_target_pairs={{4,8},{8,12},{5,9},{9,13},{6,10},{10,14},{7,11},{11,15},{20,24},{2... | collective-permute-start | bytes 393224 | tf_op jit(solution)/shard_map/ppermute | solution.py:232
  35.5 1.2 %step.23 = (f32[640,128]{1,0:T(8,128)S(1)}, f32[640,128]{1,0:T(8,128)S(1)}, f32[640,128]{1,0:T(8,128)S(1)}, f32[640,128]{1,0:T(8,128)S(1)}, f32[640,128]{1,0:T(8,128)S(1)}) custom-call(bf16[640,2048]{1,0:T(8,128)(2,1)S(1)} %copy-done.3, bf16[640,2048]{1,0:T(8,128)(2,1)S(1)} %copy-done.1, bf16[640,2048]{1,0:T(8,128)(2,1)S(1)} %copy-done.2, ...), custom_call_target="tpu_custom_call" | custom-call | flops 461373440 | bytes 100000 | tf_op jit(solution)/shard_map/step/pallas_call | solution.py:146
  36.7 1.7 %collective-permute-done.8.refs_0_.refs_5_.refs_4_ = f32[2,128,128]{2,1,0:T(8,128)S(1)} collective-permute-done((f32[2,128,128]{2,1,0:T(8,128)S(1)}, f32[2,128,128]{2,1,0:T(8,128)S(1)}, u32[]{:S(2)}, u32[]{:S(2)}) %collective-permute-start.8) | collective-permute-done | bytes 131104 | tf_op jit(solution)/shard_map/ppermute | solution.py:232
  38.5 1.3 %collective-permute-start.10 = (f32[2,128,128]{2,1,0:T(8,128)S(1)}, f32[2,128,128]{2,1,0:T(8,128)S(1)}, u32[]{:S(2)}, u32[]{:S(2)}) collective-permute-start(f32[2,128,128]{2,1,0:T(8,128)S(1)} %merge.20.refs_9_), channel_id=1, source_target_pairs={{8,12},{9,13},{10,14},{11,15},{24,28},{25,29},{26,30},{27,31}} | collective-permute-start | bytes 393224 | tf_op jit(solution)/shard_map/ppermute | solution.py:232
  39.8 0.7 %step.24 = (f32[640,128]{1,0:T(8,128)S(1)}, f32[640,128]{1,0:T(8,128)S(1)}, f32[640,128]{1,0:T(8,128)S(1)}, f32[640,128]{1,0:T(8,128)S(1)}) custom-call(bf16[640,2048]{1,0:T(8,128)(2,1)S(1)} %copy-done.3, bf16[640,2048]{1,0:T(8,128)(2,1)S(1)} %copy-done.1, bf16[640,2048]{1,0:T(8,128)(2,1)S(1)} %copy-done.2, ...), custom_call_target="tpu_custom_call" | custom-call | flops 251658240 | bytes 100000 | tf_op jit(solution)/shard_map/step/pallas_call | solution.py:146
  40.5 0.7 %collective-permute-done.9.refs_0_.refs_5_.refs_4_ = f32[2,128,128]{2,1,0:T(8,128)S(1)} collective-permute-done((f32[2,128,128]{2,1,0:T(8,128)S(1)}, f32[2,128,128]{2,1,0:T(8,128)S(1)}, u32[]{:S(2)}, u32[]{:S(2)}) %collective-permute-start.9) | collective-permute-done | bytes 131104 | tf_op jit(solution)/shard_map/ppermute | solution.py:232
  41.2 1.3 %collective-permute-start.11 = (f32[2,128,128]{2,1,0:T(8,128)S(1)}, f32[2,128,128]{2,1,0:T(8,128)S(1)}, u32[]{:S(2)}, u32[]{:S(2)}) collective-permute-start(f32[2,128,128]{2,1,0:T(8,128)S(1)} %merge.21.refs_9_), channel_id=1, source_target_pairs={{8,12},{9,13},{10,14},{11,15},{24,28},{25,29},{26,30},{27,31}} | collective-permute-start | bytes 393224 | tf_op jit(solution)/shard_map/ppermute | solution.py:232
  42.5 0.7 %step.25 = (f32[640,128]{1,0:T(8,128)S(1)}, f32[640,128]{1,0:T(8,128)S(1)}, f32[640,128]{1,0:T(8,128)S(1)}, f32[640,128]{1,0:T(8,128)S(1)}) custom-call(bf16[640,2048]{1,0:T(8,128)(2,1)S(1)} %copy-done.3, bf16[640,2048]{1,0:T(8,128)(2,1)S(1)} %copy-done.1, bf16[640,2048]{1,0:T(8,128)(2,1)S(1)} %copy-done.2, ...), custom_call_target="tpu_custom_call" | custom-call | flops 251658240 | bytes 100000 | tf_op jit(solution)/shard_map/step/pallas_call | solution.py:146
  43.3 2.1 %collective-permute-done.10.refs_5_ = f32[2,128,128]{2,1,0:T(8,128)S(1)} collective-permute-done((f32[2,128,128]{2,1,0:T(8,128)S(1)}, f32[2,128,128]{2,1,0:T(8,128)S(1)}, u32[]{:S(2)}, u32[]{:S(2)}) %collective-permute-start.10) | collective-permute-done | bytes 131104 | tf_op jit(solution)/shard_map/ppermute | solution.py:232
  45.3 0.2 step.26
  45.6 2.5 %collective-permute-done.11.refs_5_ = f32[2,128,128]{2,1,0:T(8,128)S(1)} collective-permute-done((f32[2,128,128]{2,1,0:T(8,128)S(1)}, f32[2,128,128]{2,1,0:T(8,128)S(1)}, u32[]{:S(2)}, u32[]{:S(2)}) %collective-permute-start.11) | collective-permute-done | bytes 131104 | tf_op jit(solution)/shard_map/ppermute | solution.py:232
  48.1 0.0 copy-start.4
  48.1 0.3 step.27
  48.5 0.1 collective-permute-start.12
  48.5 1.1 %collective-permute-done.12 = f32[1,640]{1,0:T(1,128)S(1)} collective-permute-done((f32[1,640]{1,0:T(1,128)S(1)}, f32[1,640]{1,0:T(1,128)S(1)}, u32[]{:S(2)}, u32[]{:S(2)}) %collective-permute-start.12) | collective-permute-done | bytes 2592 | tf_op jit(solution)/shard_map/ppermute | solution.py:208
  49.7 1.5 %collective-permute-start.13 = (f32[1,640]{1,0:T(1,128)S(1)}, f32[1,640]{1,0:T(1,128)S(1)}, u32[]{:S(2)}, u32[]{:S(2)}) collective-permute-start(f32[1,640]{1,0:T(1,128)S(1)} %add.6), channel_id=1, source_target_pairs={{0,2},{1,3},{2,0},{3,1},{4,6},{5,7},{6,4},{7,5},{8,10},{9,11},{10,... | collective-permute-start | bytes 7688 | tf_op jit(solution)/shard_map/ppermute | solution.py:208
  51.1 0.0 copy-done.4
  51.2 2.1 %collective-permute-done.13 = f32[1,640]{1,0:T(1,128)S(1)} collective-permute-done((f32[1,640]{1,0:T(1,128)S(1)}, f32[1,640]{1,0:T(1,128)S(1)}, u32[]{:S(2)}, u32[]{:S(2)}) %collective-permute-start.13) | collective-permute-done | bytes 2592 | tf_op jit(solution)/shard_map/ppermute | solution.py:208
  53.3 2.2 %finish.1 = bf16[640,2048]{1,0:T(8,128)(2,1)} custom-call(f32[640,128]{1,0:T(8,128)S(1)} %get-tuple-element.57.refs_0_, f32[640,128]{1,0:T(8,128)S(1)} %get-tuple-element.58.refs_1_, f32[640,128]{1,0:T(8,128)S(1)} %get-tuple-element.62.refs_2_, f32[640,128]{1,0:T(8,128)S(1)} %get-tuple-element.63.refs_3_, f32[640,128]{1,0:T(8,128)S(1)} %get-tuple-element.67.refs_4_, ...), custom_call_target="tpu_custom_call" | custom-call | tf_op jit(solution)/shard_map/finish/pallas_call | solution.py:189
  (14 shorter events, 0.3 us)
Async XLA Ops:
  0.0 1.7 %copy-start = (bf16[640,2048]{1,0:T(8,128)(2,1)S(1)}, bf16[640,2048]{1,0:T(8,128)(2,1)}, u32[]{:S(2)}) copy-start(bf16[640,2048]{1,0:T(8,128)(2,1)} %refs_1_.27) | copy-start | bytes 7864324
  1.7 1.7 %copy-start.2 = (bf16[640,2048]{1,0:T(8,128)(2,1)S(1)}, bf16[640,2048]{1,0:T(8,128)(2,1)}, u32[]{:S(2)}) copy-start(bf16[640,2048]{1,0:T(8,128)(2,1)} %refs_2_.27) | copy-start | bytes 7864324
  3.5 1.7 %copy-start.3 = (bf16[640,2048]{1,0:T(8,128)(2,1)S(1)}, bf16[640,2048]{1,0:T(8,128)(2,1)}, u32[]{:S(2)}) copy-start(bf16[640,2048]{1,0:T(8,128)(2,1)} %refs_0_.27) | copy-start | bytes 7864324
  3.8 3.9 %copy-start.1 = (bf16[640,2048]{1,0:T(8,128)(2,1)S(1)}, bf16[640,2048]{1,0:T(8,128)(2,1)}, u32[]{:S(2)}) copy-start(bf16[640,2048]{1,0:T(8,128)(2,1)} %refs_1_.27) | copy-start | bytes 7864324
  3.8 4.5 %collective-permute-start = (f32[2,128,128]{2,1,0:T(8,128)S(1)}, f32[2,128,128]{2,1,0:T(8,128)S(1)}, u32[]{:S(2)}, u32[]{:S(2)}) collective-permute-start(f32[2,128,128]{2,1,0:T(8,128)S(1)} %first_state.1.refs_3_.refs_4_.refs_2_), channel_id=1, source_target_pairs={{0,4},{1,5},{2,6},{3,7},{16,20},{17,21},{18,22},{19,23}} | collective-permute-start | bytes 393224 | tf_op jit(solution)/shard_map/ppermute | solution.py:232
  7.0 2.7 %collective-permute-start.2 = (f32[2,128,128]{2,1,0:T(8,128)S(1)}, f32[2,128,128]{2,1,0:T(8,128)S(1)}, u32[]{:S(2)}, u32[]{:S(2)}) collective-permute-start(f32[2,128,128]{2,1,0:T(8,128)S(1)} %merge.11.refs_3_), channel_id=1, source_target_pairs={{0,4},{1,5},{2,6},{3,7},{16,20},{17,21},{18,22},{19,23}} | collective-permute-start | bytes 393224 | tf_op jit(solution)/shard_map/ppermute | solution.py:232
  8.4 3.1 %collective-permute-start.1 = (f32[2,128,128]{2,1,0:T(8,128)S(1)}, f32[2,128,128]{2,1,0:T(8,128)S(1)}, u32[]{:S(2)}, u32[]{:S(2)}) collective-permute-start(f32[2,128,128]{2,1,0:T(8,128)S(1)} %merge.12.refs_3_), channel_id=1, source_target_pairs={{0,4},{4,8},{1,5},{5,9},{2,6},{6,10},{3,7},{7,11},{16,20},{20,24},... | collective-permute-start | bytes 393224 | tf_op jit(solution)/shard_map/ppermute | solution.py:232
  9.8 3.8 %collective-permute-start.4 = (f32[2,128,128]{2,1,0:T(8,128)S(1)}, f32[2,128,128]{2,1,0:T(8,128)S(1)}, u32[]{:S(2)}, u32[]{:S(2)}) collective-permute-start(f32[2,128,128]{2,1,0:T(8,128)S(1)} %merge.13.refs_3_), channel_id=1, source_target_pairs={{0,4},{4,8},{1,5},{5,9},{2,6},{6,10},{3,7},{7,11},{16,20},{20,24},... | collective-permute-start | bytes 393224 | tf_op jit(solution)/shard_map/ppermute | solution.py:232
  11.6 11.2 %collective-permute-start.3 = (f32[2,128,128]{2,1,0:T(8,128)S(1)}, f32[2,128,128]{2,1,0:T(8,128)S(1)}, u32[]{:S(2)}, u32[]{:S(2)}) collective-permute-start(f32[2,128,128]{2,1,0:T(8,128)S(1)} %merge.14.refs_3_), channel_id=1, source_target_pairs={{0,4},{4,8},{8,12},{1,5},{5,9},{9,13},{2,6},{6,10},{10,14},{3,7},{... | collective-permute-start | bytes 393224 | tf_op jit(solution)/shard_map/ppermute | solution.py:232
  13.6 12.4 %collective-permute-start.5 = (f32[2,128,128]{2,1,0:T(8,128)S(1)}, f32[2,128,128]{2,1,0:T(8,128)S(1)}, u32[]{:S(2)}, u32[]{:S(2)}) collective-permute-start(f32[2,128,128]{2,1,0:T(8,128)S(1)} %merge.15.refs_3_), channel_id=1, source_target_pairs={{0,4},{4,8},{8,12},{1,5},{5,9},{9,13},{2,6},{6,10},{10,14},{3,7},{... | collective-permute-start | bytes 393224 | tf_op jit(solution)/shard_map/ppermute | solution.py:232
  22.9 8.2 %collective-permute-start.6 = (f32[2,128,128]{2,1,0:T(8,128)S(1)}, f32[2,128,128]{2,1,0:T(8,128)S(1)}, u32[]{:S(2)}, u32[]{:S(2)}) collective-permute-start(f32[2,128,128]{2,1,0:T(8,128)S(1)} %merge.16.refs_8_), channel_id=1, source_target_pairs={{0,4},{4,8},{8,12},{1,5},{5,9},{9,13},{2,6},{6,10},{10,14},{3,7},{... | collective-permute-start | bytes 393224 | tf_op jit(solution)/shard_map/ppermute | solution.py:232
  26.0 8.2 %collective-permute-start.7 = (f32[2,128,128]{2,1,0:T(8,128)S(1)}, f32[2,128,128]{2,1,0:T(8,128)S(1)}, u32[]{:S(2)}, u32[]{:S(2)}) collective-permute-start(f32[2,128,128]{2,1,0:T(8,128)S(1)} %merge.17.refs_9_), channel_id=1, source_target_pairs={{0,4},{4,8},{8,12},{1,5},{5,9},{9,13},{2,6},{6,10},{10,14},{3,7},{... | collective-permute-start | bytes 393224 | tf_op jit(solution)/shard_map/ppermute | solution.py:232
  31.1 7.4 %collective-permute-start.8 = (f32[2,128,128]{2,1,0:T(8,128)S(1)}, f32[2,128,128]{2,1,0:T(8,128)S(1)}, u32[]{:S(2)}, u32[]{:S(2)}) collective-permute-start(f32[2,128,128]{2,1,0:T(8,128)S(1)} %merge.18.refs_9_), channel_id=1, source_target_pairs={{4,8},{8,12},{5,9},{9,13},{6,10},{10,14},{7,11},{11,15},{20,24},{2... | collective-permute-start | bytes 393224 | tf_op jit(solution)/shard_map/ppermute | solution.py:232
  34.2 7.0 %collective-permute-start.9 = (f32[2,128,128]{2,1,0:T(8,128)S(1)}, f32[2,128,128]{2,1,0:T(8,128)S(1)}, u32[]{:S(2)}, u32[]{:S(2)}) collective-permute-start(f32[2,128,128]{2,1,0:T(8,128)S(1)} %merge.19.refs_9_), channel_id=1, source_target_pairs={{4,8},{8,12},{5,9},{9,13},{6,10},{10,14},{7,11},{11,15},{20,24},{2... | collective-permute-start | bytes 393224 | tf_op jit(solution)/shard_map/ppermute | solution.py:232
  38.5 6.9 %collective-permute-start.10 = (f32[2,128,128]{2,1,0:T(8,128)S(1)}, f32[2,128,128]{2,1,0:T(8,128)S(1)}, u32[]{:S(2)}, u32[]{:S(2)}) collective-permute-start(f32[2,128,128]{2,1,0:T(8,128)S(1)} %merge.20.refs_9_), channel_id=1, source_target_pairs={{8,12},{9,13},{10,14},{11,15},{24,28},{25,29},{26,30},{27,31}} | collective-permute-start | bytes 393224 | tf_op jit(solution)/shard_map/ppermute | solution.py:232
  41.2 6.9 %collective-permute-start.11 = (f32[2,128,128]{2,1,0:T(8,128)S(1)}, f32[2,128,128]{2,1,0:T(8,128)S(1)}, u32[]{:S(2)}, u32[]{:S(2)}) collective-permute-start(f32[2,128,128]{2,1,0:T(8,128)S(1)} %merge.21.refs_9_), channel_id=1, source_target_pairs={{8,12},{9,13},{10,14},{11,15},{24,28},{25,29},{26,30},{27,31}} | collective-permute-start | bytes 393224 | tf_op jit(solution)/shard_map/ppermute | solution.py:232
  48.1 3.0 %copy-start.4 = (bf16[2048]{0:T(1024)(128)(2,1)S(1)}, bf16[2048]{0:T(1024)(128)(2,1)}, u32[]{:S(2)}) copy-start(bf16[2048]{0:T(1024)(128)(2,1)} %param.7) | copy-start | bytes 12292
  48.5 1.2 %collective-permute-start.12 = (f32[1,640]{1,0:T(1,128)S(1)}, f32[1,640]{1,0:T(1,128)S(1)}, u32[]{:S(2)}, u32[]{:S(2)}) collective-permute-start(f32[1,640]{1,0:T(1,128)S(1)} %get-tuple-element.90), channel_id=1, source_target_pairs={{0,1},{1,0},{2,3},{3,2},{4,5},{5,4},{6,7},{7,6},{8,9},{9,8},{10,11... | collective-permute-start | bytes 7688 | tf_op jit(solution)/shard_map/ppermute | solution.py:208
  49.7 3.6 %collective-permute-start.13 = (f32[1,640]{1,0:T(1,128)S(1)}, f32[1,640]{1,0:T(1,128)S(1)}, u32[]{:S(2)}, u32[]{:S(2)}) collective-permute-start(f32[1,640]{1,0:T(1,128)S(1)} %add.6), channel_id=1, source_target_pairs={{0,2},{1,3},{2,0},{3,1},{4,6},{5,7},{6,4},{7,5},{8,10},{9,11},{10,... | collective-permute-start | bytes 7688 | tf_op jit(solution)/shard_map/ppermute | solution.py:208

commit v2 on v0

v2 whole, which is shorter than its diff:
```python
import functools

import jax
import jax.numpy as jnp
from jax import lax
from jax.experimental import pallas as pl
from jax.experimental.pallas import tpu as pltpu
from jax.sharding import PartitionSpec as P

HEAD_DIM = 128
CHUNKS = 5
INTRA = 5
AHEAD = 3
ROUND = 1
TRAIL = 2
FIRST_COST = 1000
LOAD_COST = 1000
STATES_COST = 100000000
MERGE_COST = 1000
WORK_COST = 200000000
F32 = jnp.float32
BF16 = jnp.bfloat16
NT = ((1,), (1,))
NN = ((1,), (0,))
TN = ((0,), (0,))
VMEM = pl.BlockSpec(memory_space=pltpu.VMEM)
ANY = pl.BlockSpec(memory_space=pl.ANY)
HBM = pl.BlockSpec(memory_space=pltpu.HBM)
PARAMS = pltpu.CompilerParams(vmem_limit_bytes=12 << 20)


def cost(flops):
    return pl.CostEstimate(flops=flops, bytes_accessed=1000, transcendentals=0)


def dot(a, b, dims):
    return lax.dot_general(a, b, (dims, ((), ())), preferred_element_type=F32)


def head_columns(head):
    return slice(head * HEAD_DIM, (head + 1) * HEAD_DIM)


class Layout:
    def __init__(self, heads):
        self.heads = heads
        tiles = heads * HEAD_DIM // 8
        self.chunks = min(CHUNKS, heads)
        self.edges = [8 * (tiles * c // self.chunks) for c in range(self.chunks + 1)]

    def shape(self, chunk):
        return jax.ShapeDtypeStruct((self.edges[chunk + 1] - self.edges[chunk], HEAD_DIM), F32)

    def pieces(self, head):
        low, high = head * HEAD_DIM, (head + 1) * HEAD_DIM
        found = []
        for c in range(self.chunks):
            a, b = max(low, self.edges[c]), min(high, self.edges[c + 1])
            if a < b:
                start = self.edges[c]
                found.append((c, slice(a - start, b - start), slice(a - low, b - low)))
        return found

    def heads_of(self, chunk):
        return [h for h in range(self.heads) if any(p[0] == chunk for p in self.pieces(h))]

    def complete_with(self, chunk):
        return [h for h in range(self.heads) if self.pieces(h)[-1][0] == chunk]


def put_states(layout, heads, k_ref, v_ref, outs):
    for head in heads:
        pieces = [piece for piece in layout.pieces(head) if piece[0] in outs]
        if pieces:
            state = dot(k_ref[:, head_columns(head)], v_ref[:, head_columns(head)], TN)
            for c, rows, own in pieces:
                outs[c][rows, :] = state[own, :]


def first_body(layout, k_hbm, v_hbm, out_ref, k_buf, v_buf, sems):
    wide = k_buf.shape[1]
    copies = [
        pltpu.make_async_copy(ref.at[:, :wide], buf, sems.at[at])
        for at, (ref, buf) in enumerate(((k_hbm, k_buf), (v_hbm, v_buf)))
    ]
    for copy in copies:
        copy.start()
    for copy in copies:
        copy.wait()
    put_states(layout, layout.heads_of(0), k_buf, v_buf, {0: out_ref})


def in_hbm(*arrays):
    return [pltpu.with_memory_space_constraint(array, pltpu.HBM) for array in arrays]


def first_states(layout, keys, values):
    wide = len(layout.heads_of(0)) * HEAD_DIM
    return pl.pallas_call(
        functools.partial(first_body, layout),
        out_shape=layout.shape(0),
        in_specs=[HBM, HBM],
        out_specs=VMEM,
        scratch_shapes=[
            pltpu.VMEM((keys.shape[0], wide), BF16),
            pltpu.VMEM((keys.shape[0], wide), BF16),
            pltpu.SemaphoreType.DMA((2,)),
        ],
        compiler_params=PARAMS,
        cost_estimate=cost(FIRST_COST),
        name="first",
    )(*in_hbm(keys, values))


def load_body(layout, groups, k_hbm, v_hbm, q_hbm, order_ref, k_ref, v_ref, q_ref, out_ref, sems):
    wide = k_ref.shape[1] // groups
    copies = []
    for at in range(groups):
        cols = slice(at * wide, (at + 1) * wide)
        copies += [
            pltpu.make_async_copy(src.at[:, cols], dst.at[:, cols], sems.at[2 * at + i])
            for i, (src, dst) in enumerate(((k_hbm, k_ref), (v_hbm, v_ref)))
        ]
    query = pltpu.make_async_copy(q_hbm, q_ref, sems.at[2 * groups])
    for copy in copies:
        copy.start()
    query.start()
    for copy in copies:
        copy.wait()
    put_states(layout, layout.heads_of(1), k_ref, v_ref, {1: out_ref})
    query.wait()


def load(layout, k, v, q, order):
    groups = 4
    return pl.pallas_call(
        functools.partial(load_body, layout, groups),
        out_shape=(
            jax.ShapeDtypeStruct(k.shape, k.dtype),
            jax.ShapeDtypeStruct(v.shape, v.dtype),
            jax.ShapeDtypeStruct(q.shape, q.dtype),
            layout.shape(1),
        ),
        in_specs=[HBM] * 3 + [ANY],
        out_specs=(VMEM, VMEM, VMEM, VMEM),
        scratch_shapes=[pltpu.SemaphoreType.DMA((2 * groups + 1,))],
        compiler_params=PARAMS,
        cost_estimate=cost(LOAD_COST),
        name="load",
    )(*in_hbm(k, v, q), order)


def states_body(layout, chunk, k_ref, v_ref, order_ref, out_ref):
    put_states(layout, layout.heads_of(chunk), k_ref, v_ref, {chunk: out_ref})


def states_of(layout, chunk, k, v, order):
    return pl.pallas_call(
        functools.partial(states_body, layout, chunk),
        out_shape=layout.shape(chunk),
        in_specs=[VMEM] * 2 + [ANY],
        out_specs=VMEM,
        compiler_params=PARAMS,
        cost_estimate=cost(STATES_COST),
        name="states",
    )(k, v, order)


def merge_body(state_ref, received_ref, order_ref, out_ref):
    out_ref[...] = state_ref[...] + received_ref[...]


def merge(state, received, order):
    return pl.pallas_call(
        merge_body,
        out_shape=jax.ShapeDtypeStruct(state.shape, F32),
        in_specs=[VMEM, VMEM, ANY],
        out_specs=VMEM,
        compiler_params=PARAMS,
        cost_estimate=cost(MERGE_COST),
        name="merge",
    )(state, received, order)


def work_body(layout, hops, intra, inter, has_squares, final, orders, *refs):
    refs = list(refs)
    q_ref, k_ref, v_ref, gain_ref = refs[:4]
    refs = refs[4:]
    came = {}
    for c in needed(layout, inter):
        came[c] = [refs.pop(0) for _ in range(hops)]
    before = {h: refs.pop(0) for h in inter}
    squares = refs.pop(0)[...] if has_squares else None
    refs = refs[orders:]
    me = lax.axis_index("seq") if inter else None
    for head in inter:
        parts = []
        for c, rows, _ in layout.pieces(head):
            part = 0.0
            for hop in range(hops):
                part = jnp.where(me == hop + 1, came[c][hop][rows, :], part)
            parts.append(part)
        prefix = parts[0] if len(parts) == 1 else jnp.concatenate(parts, axis=0)
        mixed = before[head][...] + dot(q_ref[:, head_columns(head)], prefix.astype(BF16), NN)
        refs.pop(0)[...] = mixed * gain_ref[:, head_columns(head)].astype(F32)
        squares = mixed * mixed if squares is None else squares + mixed * mixed
    if inter:
        refs.pop(0)[...] = jnp.sum(squares.T, axis=0, keepdims=True) if final else squares
    for head in intra:
        cols = head_columns(head)
        scores = dot(q_ref[:, cols], k_ref[:, cols], NT)
        row = lax.broadcasted_iota(jnp.int32, scores.shape, 0)
        column = lax.broadcasted_iota(jnp.int32, scores.shape, 1)
        scores = jnp.where(row >= column, scores, 0.0).astype(BF16)
        refs.pop(0)[...] = dot(scores, v_ref[:, cols], NN)


def needed(layout, heads):
    return sorted({p[0] for h in heads for p in layout.pieces(h)})


class Worker:
    def __init__(self, layout, hops, q, k, v, gain, states, received):
        self.layout, self.hops = layout, hops
        self.inputs = [q, k, v, gain]
        self.states = states
        self.mixed = {}
        self.squares = None
        self.received = received
        self.token = None

    def run(self, intra=(), inter=(), final=False):
        tokens = self.inputs[0].shape[0]
        wide = jax.ShapeDtypeStruct((tokens, HEAD_DIM), F32)
        args = list(self.inputs)
        for c in needed(self.layout, inter):
            args += [self.received[hop, c] for hop in range(self.hops)]
        args += [self.mixed[h] for h in inter]
        has_squares = bool(inter) and self.squares is not None
        args += [self.squares] if has_squares else []
        order = [self.token]
        out = [wide for _ in inter]
        if inter:
            out.append(jax.ShapeDtypeStruct((1, tokens), F32) if final else wide)
        out += [wide for _ in intra]
        results = pl.pallas_call(
            functools.partial(
                work_body,
                self.layout,
                self.hops,
                intra,
                inter,
                has_squares,
                final,
                len(order),
            ),
            out_shape=tuple(out),
            in_specs=[VMEM] * len(args) + [ANY] * len(order),
            out_specs=tuple(VMEM for _ in out),
            compiler_params=PARAMS,
            cost_estimate=cost(1000 + WORK_COST * (4 * len(intra) + len(inter))),
            name="work",
        )(*args, *order)
        results = list(results)
        self.token = results[-1]
        for h in inter:
            self.mixed[h] = results.pop(0)
        if inter:
            self.squares = results.pop(0)
        for h in intra:
            self.mixed[h] = results.pop(0)


def finish_body(heads, width, *refs):
    mixed = refs[:heads]
    total_ref, out_ref, buf, sems = refs[heads:]
    tokens = buf.shape[0]
    factor = lax.rsqrt(total_ref[...] / width + 1e-06)
    factor = jnp.broadcast_to(factor, (HEAD_DIM, tokens)).T
    count = sems.shape[0]
    copies = []
    for at in range(count):
        rows = slice(at * tokens // count, (at + 1) * tokens // count)
        for head in range(heads):
            cols = head_columns(head)
            buf[rows, cols] = (mixed[head][rows, :] * factor[rows, :]).astype(BF16)
        copy = pltpu.make_async_copy(buf.at[rows, :], out_ref.at[rows, :], sems.at[at])
        copy.start()
        copies.append(copy)
    for copy in copies:
        copy.wait()


def finish(mixed, total, width):
    heads = len(mixed)
    tokens = mixed[0].shape[0]
    return pl.pallas_call(
        functools.partial(finish_body, heads, float(width)),
        out_shape=jax.ShapeDtypeStruct((tokens, heads * HEAD_DIM), BF16),
        in_specs=[VMEM] * (heads + 1),
        out_specs=HBM,
        scratch_shapes=[
            pltpu.VMEM((tokens, heads * HEAD_DIM), BF16),
            pltpu.SemaphoreType.DMA((tokens // 64,)),
        ],
        compiler_params=PARAMS,
        name="finish",
    )(*mixed, total)


def sum_over_heads(part, size):
    if size & (size - 1):
        return lax.psum(part, "head")
    if ROUND == 1:
        others = [
            lax.ppermute(part, "head", [(i, i ^ reach) for i in range(size)])
            for reach in range(1, size)
        ]
        low, high = [part, *others][: size // 2], [part, *others][size // 2 :]
        return functools.reduce(jnp.add, low) + functools.reduce(jnp.add, high)
    reach = 1
    while reach < size:
        part = part + lax.ppermute(part, "head", [(i, i ^ reach) for i in range(size)])
        reach *= 2
    return part


def first_hop(shards, head_shards):
    pairs = []
    for shard in range(shards):
        for h in range(head_shards):
            there = (1 - shard, h) if shard < 2 else (shard, h ^ 1)
            pairs.append((shard * head_shards + h, there[0] * head_shards + there[1]))
    return pairs


def body(shards, head_shards, q, k, v, gain):
    heads = q.shape[1] // HEAD_DIM
    layout = Layout(heads)
    chunks = layout.chunks
    hops = shards - 1
    states = {0: first_states(layout, k, v)}
    received = {}

    def send(hop, chunk, value):
        if hop == 0 and head_shards % 2 == 0:
            pairs = first_hop(shards, head_shards)
            received[hop, chunk] = lax.ppermute(value, ("seq", "head"), pairs)
        else:
            received[hop, chunk] = lax.ppermute(value, "seq", [(hop, hop + 1)])

    send(0, 0, states[0])
    k, v, q, states[1] = load(layout, k, v, q, states[0])
    send(0, 1, states[1])
    worker = Worker(layout, hops, q, k, v, gain.reshape(1, -1), states, received)
    worker.token = states[1]

    def send_own(chunk):
        states[chunk] = worker.token = states_of(layout, chunk, k, v, worker.token)
        send(0, chunk, states[chunk])

    for c in range(2, min(AHEAD, chunks)):
        send_own(c)
    waves = chunks + TRAIL * max(0, hops - 2)
    left = list(range(heads))
    todo = list(range(chunks))
    for wave in range(waves):
        for hop in range(1, hops):
            c = wave - TRAIL * (hop - 1)
            if 0 <= c < chunks:
                worker.token = merge(states[c], received[hop - 1, c], worker.token)
                send(hop, c, worker.token)
        if wave + AHEAD < chunks:
            send_own(wave + AHEAD)
        quota = -(-len(left) // max(1, INTRA - wave))
        intra, left = left[:quota], left[quota:]
        inter = []
        c = wave - TRAIL * max(0, hops - 2) - 2
        if todo and todo[0] == c:
            inter = layout.complete_with(todo.pop(0))
        if intra or inter:
            worker.run(intra=intra, inter=inter)
    for c in todo:
        worker.run(inter=layout.complete_with(c), final=c == chunks - 1)
    total = sum_over_heads(worker.squares, head_shards)
    mixed = [worker.mixed[h] for h in range(heads)]
    return finish(mixed, total, head_shards * q.shape[1])


def solution(mesh):
    placed = (
        P(("grp", "seq"), "head"),
        P(("grp", "seq"), "head"),
        P(("grp", "seq"), "head"),
        P("head"),
    )
    shape = dict(mesh.shape)
    return jax.shard_map(
        functools.partial(body, shape["seq"], shape["head"]),
        mesh=mesh,
        in_specs=placed,
        out_specs=P(("grp", "seq"), "head"),
        check_vma=False,
    )
```

time: 132 us -> 47.7 us (0.36)
  the two profiles are of different devices: /device:TPU:0 before, /device:TPU:24 now
where the time goes in v2:
time: 47.7 us; the launch traced here: 46.9 us
  Pallas kernels  18 us (38%)
  waiting for transfers between devices  15.3 us (32%)
  starting transfers between devices  13.1 us (27%)
    ppermute x10, waiting for transfers between devices, send(): received[hop, chunk] = lax.ppermute(value, 'seq', [(hop, hop + 1)])  13.5 us
    ppermute x10, starting transfers between devices, send(): received[hop, chunk] = lax.ppermute(value, 'seq', [(hop, hop + 1)])  9.83 us
    pallas_call x9, Pallas kernels, run(): pl.pallas_call(functools.partial(work_body, self.layout, self.hops, intra...  9.63 us
    pallas_call x1, Pallas kernels, load(): pl.pallas_call(functools.partial(load_body, layout, groups), out_shape=(j...  3.47 us
    ppermute x3, starting transfers between devices, sum_over_heads(): lax.ppermute(part, 'head', [(i, i ^ reach) for i in range(size)])  1.92 us
    ppermute x3, waiting for transfers between devices, sum_over_heads(): lax.ppermute(part, 'head', [(i, i ^ reach) for i in range(size)])  1.81 us
    pallas_call x1, Pallas kernels, finish(): pl.pallas_call(functools.partial(finish_body, heads, float(width)), out_s...  1.75 us
    pallas_call x1, Pallas kernels, first_states(): pl.pallas_call(functools.partial(first_body, layout), out_shape=layout.sh...  1.69 us
  transfers between devices with their start and end apart: 18, of which 7 were waited for; matrix products, arithmetic and copies ran while one was open for 0% of the time, Pallas kernels for 30%

profile of v2, /device:TPU:24, one launch (start us, length us, event | category | flops | bytes accessed | tf_op | source)
XLA Modules:
  0.0 46.9 jit_solution(9937677404443491052)
XLA Ops:
  0.0 1.7 %first.1.order_ref.state_ref = f32[408,128]{1,0:T(8,128)S(1)} custom-call(bf16[640,2048]{1,0:T(8,128)(2,1)} %k_hbm.3, bf16[640,2048]{1,0:T(8,128)(2,1)} %v_hbm.3), custom_call_target="tpu_custom_call" | custom-call | flops 1000 | bytes 1000 | tf_op jit(solution)/shard_map/first/pallas_call | solution.py:99
  1.7 0.1 collective-permute-start
  1.8 3.5 %load.1 = (bf16[640,2048]{1,0:T(8,128)(2,1)S(1)}, bf16[640,2048]{1,0:T(8,128)(2,1)S(1)}, bf16[640,2048]{1,0:T(8,128)(2,1)S(1)}, f32[408,128]{1,0:T(8,128)S(1)}) custom-call(bf16[640,2048]{1,0:T(8,128)(2,1)} %k_hbm.3, bf16[640,2048]{1,0:T(8,128)(2,1)} %v_hbm.3, bf16[640,2048]{1,0:T(8,128)(2,1)} %q_hbm.1, f32[408,128]{1,0:T(8,128)S(1)} %first.1.order_ref.state_ref), custom_call_target="tpu_custom_call" | custom-call | flops 1000 | bytes 1000 | tf_op jit(solution)/shard_map/load/pallas_call | solution.py:136
  5.3 0.6 %collective-permute-start.3 = (f32[408,128]{1,0:T(8,128)S(1)}, f32[408,128]{1,0:T(8,128)S(1)}, u32[]{:S(2)}, u32[]{:S(2)}) collective-permute-start(f32[408,128]{1,0:T(8,128)S(1)} %get-tuple-element.49.order_ref.state_ref), channel_id=1, source_target_pairs={{0,4},{1,5},{2,6},{3,7},{4,0},{5,1},{6,2},{7,3},{8,9},{9,8},{10,11... | collective-permute-start | bytes 626696 | tf_op jit(solution)/shard_map/ppermute | solution.py:348
  5.8 0.0 copy-start
  5.8 0.4 states.3.order_ref.state_ref
  6.2 0.1 collective-permute-start.2
  6.3 0.2 copy-done
  6.5 0.0 collective-permute-done.received_ref.refs_4_
  6.5 0.4 states.4.refs_4_.state_ref
  7.0 0.7 %collective-permute-start.1 = (f32[408,128]{1,0:T(8,128)S(1)}, f32[408,128]{1,0:T(8,128)S(1)}, u32[]{:S(2)}, u32[]{:S(2)}) collective-permute-start(f32[408,128]{1,0:T(8,128)S(1)} %merge.10.order_ref), channel_id=1, source_target_pairs={{4,8},{5,9},{6,10},{7,11},{20,24},{21,25},{22,26},{23,27}} | collective-permute-start | bytes 626696 | tf_op jit(solution)/shard_map/ppermute | solution.py:350
  7.6 0.4 collective-permute-start.8
  8.0 1.9 %work.9 = (f32[640,128]{1,0:T(8,128)S(1)}, f32[640,128]{1,0:T(8,128)S(1)}, f32[640,128]{1,0:T(8,128)S(1)}, f32[640,128]{1,0:T(8,128)S(1)}) custom-call(bf16[640,2048]{1,0:T(8,128)(2,1)S(1)} %get-tuple-element.46.refs_0_, bf16[640,2048]{1,0:T(8,128)(2,1)S(1)} %get-tuple-element.47.k_ref.refs_1_, bf16[640,2048]{1,0:T(8,128)(2,1)S(1)} %get-tuple-element.48.v_ref.refs_2_, ...), custom_call_target="tpu_custom_call" | custom-call | flops 3200001024 | bytes 1000 | tf_op jit(solution)/shard_map/work/pallas_call | solution.py:246
  10.0 0.0 collective-permute-done.3.received_ref.refs_7_.refs_4_
  10.0 0.4 states.5.refs_4_.state_ref
  10.4 0.7 %collective-permute-start.7 = (f32[408,128]{1,0:T(8,128)S(1)}, f32[408,128]{1,0:T(8,128)S(1)}, u32[]{:S(2)}, u32[]{:S(2)}) collective-permute-start(f32[408,128]{1,0:T(8,128)S(1)} %merge.11.order_ref), channel_id=1, source_target_pairs={{4,8},{5,9},{6,10},{7,11},{20,24},{21,25},{22,26},{23,27}} | collective-permute-start | bytes 626696 | tf_op jit(solution)/shard_map/ppermute | solution.py:350
  11.1 0.3 collective-permute-start.6
  11.4 1.5 %work.10 = (f32[640,128]{1,0:T(8,128)S(1)}, f32[640,128]{1,0:T(8,128)S(1)}, f32[640,128]{1,0:T(8,128)S(1)}) custom-call(bf16[640,2048]{1,0:T(8,128)(2,1)S(1)} %get-tuple-element.46.refs_0_, bf16[640,2048]{1,0:T(8,128)(2,1)S(1)} %get-tuple-element.47.k_ref.refs_1_, bf16[640,2048]{1,0:T(8,128)(2,1)S(1)} %get-tuple-element.48.v_ref.refs_2_, ...), custom_call_target="tpu_custom_call" | custom-call | flops 2400001024 | bytes 1000 | tf_op jit(solution)/shard_map/work/pallas_call | solution.py:246
  12.9 0.0 collective-permute-done.2.received_ref.refs_7_.refs_4_
  12.9 0.7 %collective-permute-start.5 = (f32[408,128]{1,0:T(8,128)S(1)}, f32[408,128]{1,0:T(8,128)S(1)}, u32[]{:S(2)}, u32[]{:S(2)}) collective-permute-start(f32[408,128]{1,0:T(8,128)S(1)} %merge.12.order_ref), channel_id=1, source_target_pairs={{4,8},{5,9},{6,10},{7,11},{20,24},{21,25},{22,26},{23,27}} | collective-permute-start | bytes 626696 | tf_op jit(solution)/shard_map/ppermute | solution.py:350
  13.6 0.0 collective-permute-done.1.received_ref.refs_5_
  13.7 1.3 %collective-permute-start.4 = (f32[408,128]{1,0:T(8,128)S(1)}, f32[408,128]{1,0:T(8,128)S(1)}, u32[]{:S(2)}, u32[]{:S(2)}) collective-permute-start(f32[408,128]{1,0:T(8,128)S(1)} %merge.13.refs_4_), channel_id=1, source_target_pairs={{8,12},{9,13},{10,14},{11,15},{24,28},{25,29},{26,30},{27,31}} | collective-permute-start | bytes 626696 | tf_op jit(solution)/shard_map/ppermute | solution.py:350
  15.0 1.5 %work.11 = (f32[640,128]{1,0:T(8,128)S(1)}, f32[640,128]{1,0:T(8,128)S(1)}, f32[640,128]{1,0:T(8,128)S(1)}) custom-call(bf16[640,2048]{1,0:T(8,128)(2,1)S(1)} %get-tuple-element.46.refs_0_, bf16[640,2048]{1,0:T(8,128)(2,1)S(1)} %get-tuple-element.47.k_ref.refs_1_, bf16[640,2048]{1,0:T(8,128)(2,1)S(1)} %get-tuple-element.48.v_ref.refs_2_, ...), custom_call_target="tpu_custom_call" | custom-call | flops 2400001024 | bytes 1000 | tf_op jit(solution)/shard_map/work/pallas_call | solution.py:246
  16.5 0.0 collective-permute-done.8.received_ref.refs_7_.refs_4_
  16.5 0.7 %collective-permute-start.10 = (f32[408,128]{1,0:T(8,128)S(1)}, f32[408,128]{1,0:T(8,128)S(1)}, u32[]{:S(2)}, u32[]{:S(2)}) collective-permute-start(f32[408,128]{1,0:T(8,128)S(1)} %merge.14.order_ref), channel_id=1, source_target_pairs={{4,8},{5,9},{6,10},{7,11},{20,24},{21,25},{22,26},{23,27}} | collective-permute-start | bytes 626696 | tf_op jit(solution)/shard_map/ppermute | solution.py:350
  17.2 0.0 collective-permute-done.7.received_ref.refs_8_.refs_5_
  17.2 1.3 %collective-permute-start.9 = (f32[408,128]{1,0:T(8,128)S(1)}, f32[408,128]{1,0:T(8,128)S(1)}, u32[]{:S(2)}, u32[]{:S(2)}) collective-permute-start(f32[408,128]{1,0:T(8,128)S(1)} %merge.15.refs_4_), channel_id=1, source_target_pairs={{8,12},{9,13},{10,14},{11,15},{24,28},{25,29},{26,30},{27,31}} | collective-permute-start | bytes 626696 | tf_op jit(solution)/shard_map/ppermute | solution.py:350
  18.5 1.5 %work.12 = (f32[640,128]{1,0:T(8,128)S(1)}, f32[640,128]{1,0:T(8,128)S(1)}, f32[640,128]{1,0:T(8,128)S(1)}) custom-call(bf16[640,2048]{1,0:T(8,128)(2,1)S(1)} %get-tuple-element.46.refs_0_, bf16[640,2048]{1,0:T(8,128)(2,1)S(1)} %get-tuple-element.47.k_ref.refs_1_, bf16[640,2048]{1,0:T(8,128)(2,1)S(1)} %get-tuple-element.48.v_ref.refs_2_, ...), custom_call_target="tpu_custom_call" | custom-call | flops 2400001024 | bytes 1000 | tf_op jit(solution)/shard_map/work/pallas_call | solution.py:246
  20.1 0.0 collective-permute-done.6.received_ref.refs_7_
  20.1 0.7 %collective-permute-start.12 = (f32[416,128]{1,0:T(8,128)S(1)}, f32[416,128]{1,0:T(8,128)S(1)}, u32[]{:S(2)}, u32[]{:S(2)}) collective-permute-start(f32[416,128]{1,0:T(8,128)S(1)} %merge.16.order_ref), channel_id=1, source_target_pairs={{4,8},{5,9},{6,10},{7,11},{20,24},{21,25},{22,26},{23,27}} | collective-permute-start | bytes 638984 | tf_op jit(solution)/shard_map/ppermute | solution.py:350
  20.8 0.0 collective-permute-done.5.received_ref.refs_8_.refs_5_
  20.8 1.3 %collective-permute-start.11 = (f32[408,128]{1,0:T(8,128)S(1)}, f32[408,128]{1,0:T(8,128)S(1)}, u32[]{:S(2)}, u32[]{:S(2)}) collective-permute-start(f32[408,128]{1,0:T(8,128)S(1)} %merge.17.refs_10_), channel_id=1, source_target_pairs={{8,12},{9,13},{10,14},{11,15},{24,28},{25,29},{26,30},{27,31}} | collective-permute-start | bytes 626696 | tf_op jit(solution)/shard_map/ppermute | solution.py:350
  22.1 1.0 %collective-permute-done.4.refs_6_ = f32[408,128]{1,0:T(8,128)S(1)} collective-permute-done((f32[408,128]{1,0:T(8,128)S(1)}, f32[408,128]{1,0:T(8,128)S(1)}, u32[]{:S(2)}, u32[]{:S(2)}) %collective-permute-start.4) | collective-permute-done | bytes 208928 | tf_op jit(solution)/shard_map/ppermute | solution.py:350
  23.1 1.7 %work.13 = (f32[640,128]{1,0:T(8,128)S(1)}, f32[640,128]{1,0:T(8,128)S(1)}, f32[640,128]{1,0:T(8,128)S(1)}, f32[640,128]{1,0:T(8,128)S(1)}, f32[640,128]{1,0:T(8...) custom-call(bf16[640,2048]{1,0:T(8,128)(2,1)S(1)} %get-tuple-element.46.refs_0_, ...), custom_call_target="tpu_custom_call" | custom-call | flops 3000001024 | bytes 1000 | tf_op jit(solution)/shard_map/work/pallas_call | solution.py:246
  24.8 0.0 collective-permute-done.10.received_ref.refs_8_.refs_5_
  24.8 1.3 %collective-permute-start.13 = (f32[408,128]{1,0:T(8,128)S(1)}, f32[408,128]{1,0:T(8,128)S(1)}, u32[]{:S(2)}, u32[]{:S(2)}) collective-permute-start(f32[408,128]{1,0:T(8,128)S(1)} %merge.18.refs_14_), channel_id=1, source_target_pairs={{8,12},{9,13},{10,14},{11,15},{24,28},{25,29},{26,30},{27,31}} | collective-permute-start | bytes 626696 | tf_op jit(solution)/shard_map/ppermute | solution.py:350
  26.1 1.8 %collective-permute-done.9.refs_9_.refs_6_ = f32[408,128]{1,0:T(8,128)S(1)} collective-permute-done((f32[408,128]{1,0:T(8,128)S(1)}, f32[408,128]{1,0:T(8,128)S(1)}, u32[]{:S(2)}, u32[]{:S(2)}) %collective-permute-start.9) | collective-permute-done | bytes 208928 | tf_op jit(solution)/shard_map/ppermute | solution.py:350
  27.9 0.3 work.14
  28.2 0.0 collective-permute-done.12.received_ref.refs_8_
  28.2 1.3 %collective-permute-start.14 = (f32[416,128]{1,0:T(8,128)S(1)}, f32[416,128]{1,0:T(8,128)S(1)}, u32[]{:S(2)}, u32[]{:S(2)}) collective-permute-start(f32[416,128]{1,0:T(8,128)S(1)} %merge.19.refs_14_), channel_id=1, source_target_pairs={{8,12},{9,13},{10,14},{11,15},{24,28},{25,29},{26,30},{27,31}} | collective-permute-start | bytes 638984 | tf_op jit(solution)/shard_map/ppermute | solution.py:350
  29.5 3.0 %collective-permute-done.11.refs_9_.refs_6_ = f32[408,128]{1,0:T(8,128)S(1)} collective-permute-done((f32[408,128]{1,0:T(8,128)S(1)}, f32[408,128]{1,0:T(8,128)S(1)}, u32[]{:S(2)}, u32[]{:S(2)}) %collective-permute-start.11) | collective-permute-done | bytes 208928 | tf_op jit(solution)/shard_map/ppermute | solution.py:350
  32.5 0.3 work.15
  32.8 4.0 %collective-permute-done.13.refs_9_.refs_6_ = f32[408,128]{1,0:T(8,128)S(1)} collective-permute-done((f32[408,128]{1,0:T(8,128)S(1)}, f32[408,128]{1,0:T(8,128)S(1)}, u32[]{:S(2)}, u32[]{:S(2)}) %collective-permute-start.13) | collective-permute-done | bytes 208928 | tf_op jit(solution)/shard_map/ppermute | solution.py:350
  36.8 0.3 work.16
  37.1 3.8 %collective-permute-done.14.refs_9_ = f32[416,128]{1,0:T(8,128)S(1)} collective-permute-done((f32[416,128]{1,0:T(8,128)S(1)}, f32[416,128]{1,0:T(8,128)S(1)}, u32[]{:S(2)}, u32[]{:S(2)}) %collective-permute-start.14) | collective-permute-done | bytes 213024 | tf_op jit(solution)/shard_map/ppermute | solution.py:350
  40.9 0.5 %work.17 = (f32[640,128]{1,0:T(8,128)S(1)}, f32[640,128]{1,0:T(8,128)S(1)}, f32[640,128]{1,0:T(8,128)S(1)}, f32[640,128]{1,0:T(8,128)S(1)}, f32[1,640]{1,0:T(1,128)S(1)}) custom-call(bf16[640,2048]{1,0:T(8,128)(2,1)S(1)} %get-tuple-element.46.refs_0_, bf16[640,2048]{1,0:T(8,128)(2,1)S(1)} %get-tuple-element.47.k_ref.refs_1_, ...), custom_call_target="tpu_custom_call" | custom-call | flops 800001024 | bytes 1000 | tf_op jit(solution)/shard_map/work/pallas_call | solution.py:246
  41.4 0.1 collective-permute-start.17
  41.5 1.5 %collective-permute-start.16 = (f32[1,640]{1,0:T(1,128)S(1)}, f32[1,640]{1,0:T(1,128)S(1)}, u32[]{:S(2)}, u32[]{:S(2)}) collective-permute-start(f32[1,640]{1,0:T(1,128)S(1)} %get-tuple-element.86), channel_id=1, source_target_pairs={{0,2},{1,3},{2,0},{3,1},{4,6},{5,7},{6,4},{7,5},{8,10},{9,11},{10,... | collective-permute-start | bytes 7688 | tf_op jit(solution)/shard_map/ppermute | solution.py:316
  43.0 0.3 collective-permute-start.15
  43.3 1.2 %collective-permute-done.17 = f32[1,640]{1,0:T(1,128)S(1)} collective-permute-done((f32[1,640]{1,0:T(1,128)S(1)}, f32[1,640]{1,0:T(1,128)S(1)}, u32[]{:S(2)}, u32[]{:S(2)}) %collective-permute-start.17) | collective-permute-done | bytes 2592 | tf_op jit(solution)/shard_map/ppermute | solution.py:316
  44.5 0.7 %collective-permute-done.16 = f32[1,640]{1,0:T(1,128)S(1)} collective-permute-done((f32[1,640]{1,0:T(1,128)S(1)}, f32[1,640]{1,0:T(1,128)S(1)}, u32[]{:S(2)}, u32[]{:S(2)}) %collective-permute-start.16) | collective-permute-done | bytes 2592 | tf_op jit(solution)/shard_map/ppermute | solution.py:316
  45.1 0.0 collective-permute-done.15
  45.2 1.8 %finish.1 = bf16[640,2048]{1,0:T(8,128)(2,1)} custom-call(f32[640,128]{1,0:T(8,128)S(1)} %get-tuple-element.57.refs_0_, f32[640,128]{1,0:T(8,128)S(1)} %get-tuple-element.58.refs_1_, f32[640,128]{1,0:T(8,128)S(1)} %get-tuple-element.59.refs_2_, f32[640,128]{1,0:T(8,128)S(1)} %get-tuple-element.64.refs_3_, f32[640,128]{1,0:T(8,128)S(1)} %get-tuple-element.65.refs_4_, ...), custom_call_target="tpu_custom_call" | custom-call | tf_op jit(solution)/shard_map/finish/pallas_call | solution.py:297
  (12 shorter events, 0.3 us)
Async XLA Ops:
  1.7 4.8 %collective-permute-start = (f32[408,128]{1,0:T(8,128)S(1)}, f32[408,128]{1,0:T(8,128)S(1)}, u32[]{:S(2)}, u32[]{:S(2)}) collective-permute-start(f32[408,128]{1,0:T(8,128)S(1)} %first.1.order_ref.state_ref), channel_id=1, source_target_pairs={{0,4},{1,5},{2,6},{3,7},{4,0},{5,1},{6,2},{7,3},{8,9},{9,8},{10,11... | collective-permute-start | bytes 626696 | tf_op jit(solution)/shard_map/ppermute | solution.py:348
  5.3 4.7 %collective-permute-start.3 = (f32[408,128]{1,0:T(8,128)S(1)}, f32[408,128]{1,0:T(8,128)S(1)}, u32[]{:S(2)}, u32[]{:S(2)}) collective-permute-start(f32[408,128]{1,0:T(8,128)S(1)} %get-tuple-element.49.order_ref.state_ref), channel_id=1, source_target_pairs={{0,4},{1,5},{2,6},{3,7},{4,0},{5,1},{6,2},{7,3},{8,9},{9,8},{10,11... | collective-permute-start | bytes 626696 | tf_op jit(solution)/shard_map/ppermute | solution.py:348
  5.8 0.7 %copy-start = (bf16[2048]{0:T(1024)(128)(2,1)S(1)}, bf16[2048]{0:T(1024)(128)(2,1)}, u32[]{:S(2)}) copy-start(bf16[2048]{0:T(1024)(128)(2,1)} %param.7) | copy-start | bytes 12292
  6.2 6.7 %collective-permute-start.2 = (f32[408,128]{1,0:T(8,128)S(1)}, f32[408,128]{1,0:T(8,128)S(1)}, u32[]{:S(2)}, u32[]{:S(2)}) collective-permute-start(f32[408,128]{1,0:T(8,128)S(1)} %states.3.order_ref.state_ref), channel_id=1, source_target_pairs={{0,4},{1,5},{2,6},{3,7},{4,0},{5,1},{6,2},{7,3},{8,9},{9,8},{10,11... | collective-permute-start | bytes 626696 | tf_op jit(solution)/shard_map/ppermute | solution.py:348
  7.0 6.7 %collective-permute-start.1 = (f32[408,128]{1,0:T(8,128)S(1)}, f32[408,128]{1,0:T(8,128)S(1)}, u32[]{:S(2)}, u32[]{:S(2)}) collective-permute-start(f32[408,128]{1,0:T(8,128)S(1)} %merge.10.order_ref), channel_id=1, source_target_pairs={{4,8},{5,9},{6,10},{7,11},{20,24},{21,25},{22,26},{23,27}} | collective-permute-start | bytes 626696 | tf_op jit(solution)/shard_map/ppermute | solution.py:350
  7.6 8.8 %collective-permute-start.8 = (f32[408,128]{1,0:T(8,128)S(1)}, f32[408,128]{1,0:T(8,128)S(1)}, u32[]{:S(2)}, u32[]{:S(2)}) collective-permute-start(f32[408,128]{1,0:T(8,128)S(1)} %states.4.refs_4_.state_ref), channel_id=1, source_target_pairs={{0,4},{1,5},{2,6},{3,7},{4,0},{5,1},{6,2},{7,3},{8,9},{9,8},{10,11... | collective-permute-start | bytes 626696 | tf_op jit(solution)/shard_map/ppermute | solution.py:348
  10.4 6.8 %collective-permute-start.7 = (f32[408,128]{1,0:T(8,128)S(1)}, f32[408,128]{1,0:T(8,128)S(1)}, u32[]{:S(2)}, u32[]{:S(2)}) collective-permute-start(f32[408,128]{1,0:T(8,128)S(1)} %merge.11.order_ref), channel_id=1, source_target_pairs={{4,8},{5,9},{6,10},{7,11},{20,24},{21,25},{22,26},{23,27}} | collective-permute-start | bytes 626696 | tf_op jit(solution)/shard_map/ppermute | solution.py:350
  11.1 9.0 %collective-permute-start.6 = (f32[416,128]{1,0:T(8,128)S(1)}, f32[416,128]{1,0:T(8,128)S(1)}, u32[]{:S(2)}, u32[]{:S(2)}) collective-permute-start(f32[416,128]{1,0:T(8,128)S(1)} %states.5.refs_4_.state_ref), channel_id=1, source_target_pairs={{0,4},{1,5},{2,6},{3,7},{4,0},{5,1},{6,2},{7,3},{8,9},{9,8},{10,11... | collective-permute-start | bytes 638984 | tf_op jit(solution)/shard_map/ppermute | solution.py:348
  12.9 7.9 %collective-permute-start.5 = (f32[408,128]{1,0:T(8,128)S(1)}, f32[408,128]{1,0:T(8,128)S(1)}, u32[]{:S(2)}, u32[]{:S(2)}) collective-permute-start(f32[408,128]{1,0:T(8,128)S(1)} %merge.12.order_ref), channel_id=1, source_target_pairs={{4,8},{5,9},{6,10},{7,11},{20,24},{21,25},{22,26},{23,27}} | collective-permute-start | bytes 626696 | tf_op jit(solution)/shard_map/ppermute | solution.py:350
  13.7 9.5 %collective-permute-start.4 = (f32[408,128]{1,0:T(8,128)S(1)}, f32[408,128]{1,0:T(8,128)S(1)}, u32[]{:S(2)}, u32[]{:S(2)}) collective-permute-start(f32[408,128]{1,0:T(8,128)S(1)} %merge.13.refs_4_), channel_id=1, source_target_pairs={{8,12},{9,13},{10,14},{11,15},{24,28},{25,29},{26,30},{27,31}} | collective-permute-start | bytes 626696 | tf_op jit(solution)/shard_map/ppermute | solution.py:350
  16.5 8.3 %collective-permute-start.10 = (f32[408,128]{1,0:T(8,128)S(1)}, f32[408,128]{1,0:T(8,128)S(1)}, u32[]{:S(2)}, u32[]{:S(2)}) collective-permute-start(f32[408,128]{1,0:T(8,128)S(1)} %merge.14.order_ref), channel_id=1, source_target_pairs={{4,8},{5,9},{6,10},{7,11},{20,24},{21,25},{22,26},{23,27}} | collective-permute-start | bytes 626696 | tf_op jit(solution)/shard_map/ppermute | solution.py:350
  17.2 10.6 %collective-permute-start.9 = (f32[408,128]{1,0:T(8,128)S(1)}, f32[408,128]{1,0:T(8,128)S(1)}, u32[]{:S(2)}, u32[]{:S(2)}) collective-permute-start(f32[408,128]{1,0:T(8,128)S(1)} %merge.15.refs_4_), channel_id=1, source_target_pairs={{8,12},{9,13},{10,14},{11,15},{24,28},{25,29},{26,30},{27,31}} | collective-permute-start | bytes 626696 | tf_op jit(solution)/shard_map/ppermute | solution.py:350
  20.1 8.1 %collective-permute-start.12 = (f32[416,128]{1,0:T(8,128)S(1)}, f32[416,128]{1,0:T(8,128)S(1)}, u32[]{:S(2)}, u32[]{:S(2)}) collective-permute-start(f32[416,128]{1,0:T(8,128)S(1)} %merge.16.order_ref), channel_id=1, source_target_pairs={{4,8},{5,9},{6,10},{7,11},{20,24},{21,25},{22,26},{23,27}} | collective-permute-start | bytes 638984 | tf_op jit(solution)/shard_map/ppermute | solution.py:350
  20.8 11.7 %collective-permute-start.11 = (f32[408,128]{1,0:T(8,128)S(1)}, f32[408,128]{1,0:T(8,128)S(1)}, u32[]{:S(2)}, u32[]{:S(2)}) collective-permute-start(f32[408,128]{1,0:T(8,128)S(1)} %merge.17.refs_10_), channel_id=1, source_target_pairs={{8,12},{9,13},{10,14},{11,15},{24,28},{25,29},{26,30},{27,31}} | collective-permute-start | bytes 626696 | tf_op jit(solution)/shard_map/ppermute | solution.py:350
  24.8 12.0 %collective-permute-start.13 = (f32[408,128]{1,0:T(8,128)S(1)}, f32[408,128]{1,0:T(8,128)S(1)}, u32[]{:S(2)}, u32[]{:S(2)}) collective-permute-start(f32[408,128]{1,0:T(8,128)S(1)} %merge.18.refs_14_), channel_id=1, source_target_pairs={{8,12},{9,13},{10,14},{11,15},{24,28},{25,29},{26,30},{27,31}} | collective-permute-start | bytes 626696 | tf_op jit(solution)/shard_map/ppermute | solution.py:350
  28.2 12.7 %collective-permute-start.14 = (f32[416,128]{1,0:T(8,128)S(1)}, f32[416,128]{1,0:T(8,128)S(1)}, u32[]{:S(2)}, u32[]{:S(2)}) collective-permute-start(f32[416,128]{1,0:T(8,128)S(1)} %merge.19.refs_14_), channel_id=1, source_target_pairs={{8,12},{9,13},{10,14},{11,15},{24,28},{25,29},{26,30},{27,31}} | collective-permute-start | bytes 638984 | tf_op jit(solution)/shard_map/ppermute | solution.py:350
  41.4 3.1 %collective-permute-start.17 = (f32[1,640]{1,0:T(1,128)S(1)}, f32[1,640]{1,0:T(1,128)S(1)}, u32[]{:S(2)}, u32[]{:S(2)}) collective-permute-start(f32[1,640]{1,0:T(1,128)S(1)} %get-tuple-element.86), channel_id=1, source_target_pairs={{0,3},{1,2},{2,1},{3,0},{4,7},{5,6},{6,5},{7,4},{8,11},{9,10},{10,... | collective-permute-start | bytes 7688 | tf_op jit(solution)/shard_map/ppermute | solution.py:316
  41.5 3.7 %collective-permute-start.16 = (f32[1,640]{1,0:T(1,128)S(1)}, f32[1,640]{1,0:T(1,128)S(1)}, u32[]{:S(2)}, u32[]{:S(2)}) collective-permute-start(f32[1,640]{1,0:T(1,128)S(1)} %get-tuple-element.86), channel_id=1, source_target_pairs={{0,2},{1,3},{2,0},{3,1},{4,6},{5,7},{6,4},{7,5},{8,10},{9,11},{10,... | collective-permute-start | bytes 7688 | tf_op jit(solution)/shard_map/ppermute | solution.py:316
  43.0 2.1 %collective-permute-start.15 = (f32[1,640]{1,0:T(1,128)S(1)}, f32[1,640]{1,0:T(1,128)S(1)}, u32[]{:S(2)}, u32[]{:S(2)}) collective-permute-start(f32[1,640]{1,0:T(1,128)S(1)} %get-tuple-element.86), channel_id=1, source_target_pairs={{0,1},{1,0},{2,3},{3,2},{4,5},{5,4},{6,7},{7,6},{8,9},{9,8},{10,11... | collective-permute-start | bytes 7688 | tf_op jit(solution)/shard_map/ppermute | solution.py:316

commit v3 on v2

--- a/solution.py
+++ b/solution.py
@@ -8,16 +8,20 @@
 from jax.sharding import PartitionSpec as P
 
 HEAD_DIM = 128
-CHUNKS = 5
-INTRA = 5
+CHUNKS = 6
+INTRA = 8
 AHEAD = 3
 ROUND = 1
 TRAIL = 2
+OWN = 5
+OUT_ROWS = 64
 FIRST_COST = 1000
 LOAD_COST = 1000
 STATES_COST = 100000000
 MERGE_COST = 1000
 WORK_COST = 200000000
+BYTES = 1000
+MIN_COST = 1000
 F32 = jnp.float32
 BF16 = jnp.bfloat16
 NT = ((1,), (1,))
@@ -30,7 +34,7 @@
 
 
 def cost(flops):
-    return pl.CostEstimate(flops=flops, bytes_accessed=1000, transcendentals=0)
+    return pl.CostEstimate(flops=flops, bytes_accessed=BYTES, transcendentals=0)
 
 
 def dot(a, b, dims):
@@ -46,7 +50,8 @@
         self.heads = heads
         tiles = heads * HEAD_DIM // 8
         self.chunks = min(CHUNKS, heads)
-        self.edges = [8 * (tiles * c // self.chunks) for c in range(self.chunks + 1)]
+        most = -(-tiles // self.chunks)
+        self.edges = [8 * max(0, tiles - most * (self.chunks - c)) for c in range(self.chunks + 1)]
 
     def shape(self, chunk):
         return jax.ShapeDtypeStruct((self.edges[chunk + 1] - self.edges[chunk], HEAD_DIM), F32)
@@ -167,7 +172,31 @@
 
 
 def merge_body(state_ref, received_ref, order_ref, out_ref):
-    out_ref[...] = state_ref[...] + received_ref[...]
+    out_ref[...] = state_ref[...] + received_ref[: state_ref.shape[0], :]
+
+
+def padded(value, rows):
+    lacking = rows - value.shape[0]
+    return value if lacking == 0 else jnp.pad(value, ((0, lacking), (0, 0)))
+
+
+def merge_two_body(state_ref, received_ref, late_ref, order_ref, out_ref):
+    rows = out_ref.shape[0]
+    onward = padded(state_ref[...] + received_ref[: state_ref.shape[0], :], rows)
+    out_ref[...] = jnp.where(lax.axis_index("seq") == 2, onward, padded(late_ref[...], rows))
+
+
+def merge_two(state, received, late, order):
+    rows = max(state.shape[0], late.shape[0])
+    return pl.pallas_call(
+        merge_two_body,
+        out_shape=jax.ShapeDtypeStruct((rows, HEAD_DIM), F32),
+        in_specs=[VMEM] * 3 + [ANY],
+        out_specs=VMEM,
+        compiler_params=PARAMS,
+        cost_estimate=cost(MERGE_COST),
+        name="merge_two",
+    )(state, received, late, order)
 
 
 def merge(state, received, order):
@@ -206,13 +235,26 @@
         squares = mixed * mixed if squares is None else squares + mixed * mixed
     if inter:
         refs.pop(0)[...] = jnp.sum(squares.T, axis=0, keepdims=True) if final else squares
+    tokens = q_ref.shape[0]
+    cut = tokens * 3 // 5 // HEAD_DIM * HEAD_DIM
     for head in intra:
         cols = head_columns(head)
-        scores = dot(q_ref[:, cols], k_ref[:, cols], NT)
-        row = lax.broadcasted_iota(jnp.int32, scores.shape, 0)
-        column = lax.broadcasted_iota(jnp.int32, scores.shape, 1)
-        scores = jnp.where(row >= column, scores, 0.0).astype(BF16)
-        refs.pop(0)[...] = dot(scores, v_ref[:, cols], NN)
+        out_ref = refs.pop(0)
+        late = causal(dot(q_ref[cut:, cols], k_ref[cut:, cols], NT))
+        late = dot(late, v_ref[cut:, cols], NN)
+        if cut:
+            scores = dot(q_ref[:, cols], k_ref[:cut, cols], NT)
+            scores = jnp.concatenate([causal(scores[:cut]), scores[cut:].astype(BF16)], axis=0)
+            early = dot(scores, v_ref[:cut, cols], NN)
+            out_ref[:cut, :] = early[:cut]
+            late = early[cut:] + late
+        out_ref[cut:, :] = late
+
+
+def causal(scores):
+    row = lax.broadcasted_iota(jnp.int32, scores.shape, 0)
+    column = lax.broadcasted_iota(jnp.int32, scores.shape, 1)
+    return jnp.where(row >= column, scores, 0.0).astype(BF16)
 
 
 def needed(layout, heads):
@@ -258,7 +300,7 @@
             in_specs=[VMEM] * len(args) + [ANY] * len(order),
             out_specs=tuple(VMEM for _ in out),
             compiler_params=PARAMS,
-            cost_estimate=cost(1000 + WORK_COST * (4 * len(intra) + len(inter))),
+            cost_estimate=cost(MIN_COST + WORK_COST * (4 * len(intra) + len(inter))),
             name="work",
         )(*args, *order)
         results = list(results)
@@ -301,7 +343,7 @@
         out_specs=HBM,
         scratch_shapes=[
             pltpu.VMEM((tokens, heads * HEAD_DIM), BF16),
-            pltpu.SemaphoreType.DMA((tokens // 64,)),
+            pltpu.SemaphoreType.DMA((tokens // OUT_ROWS,)),
         ],
         compiler_params=PARAMS,
         name="finish",
@@ -359,6 +401,7 @@
         states[chunk] = worker.token = states_of(layout, chunk, k, v, worker.token)
         send(0, chunk, states[chunk])
 
+    own = OWN if hops > 2 else chunks
     for c in range(2, min(AHEAD, chunks)):
         send_own(c)
     waves = chunks + TRAIL * max(0, hops - 2)
@@ -367,10 +410,18 @@
     for wave in range(waves):
         for hop in range(1, hops):
             c = wave - TRAIL * (hop - 1)
-            if 0 <= c < chunks:
+            if not 0 <= c < chunks:
+                continue
+            if hop == 2 and own + c < chunks:
+                late = own + c
+                states[late] = worker.token = states_of(layout, late, k, v, worker.token)
+                worker.token = merge_two(states[c], received[1, c], states[late], worker.token)
+                pairs = [(0, 1), (2, 3)]
+                received[2, c] = received[0, late] = lax.ppermute(worker.token, "seq", pairs)
+            else:
                 worker.token = merge(states[c], received[hop - 1, c], worker.token)
                 send(hop, c, worker.token)
-        if wave + AHEAD < chunks:
+        if wave + AHEAD < min(own, chunks):
             send_own(wave + AHEAD)
         quota = -(-len(left) // max(1, INTRA - wave))
         intra, left = left[:quota], left[quota:]

time: 47.7 us -> 47.2 us (0.990)
  waiting for transfers between devices: 15.3 us -> 12.5 us
  starting transfers between devices: 13.1 us -> 15.5 us
    ppermute x10 -> x11, waiting for transfers between devices: 13.5 us -> 9.09 us  [send(): received[hop, chunk] = lax.ppermute(value, 'seq', [(hop, hop + 1)])]
    ppermute x0 -> x1, starting transfers between devices: none -> 1.29 us  [body(): lax.ppermute(worker.token, 'seq', pairs)]
    ppermute x0 -> x1, waiting for transfers between devices: none -> 0.98 us  [body(): lax.ppermute(worker.token, 'seq', pairs)]
    ppermute x10 -> x11, starting transfers between devices: 9.83 us -> 10.7 us  [send(): received[hop, chunk] = lax.ppermute(value, 'seq', [(hop, hop + 1)])]
    ppermute x3, waiting for transfers between devices: 1.81 us -> 2.37 us  [sum_over_heads(): lax.ppermute(part, 'head', [(i, i ^ reach) for i in range(size)])]
    pallas_call x3 -> x4, Pallas kernels: 1.21 us -> 1.53 us  [states_of(): pl.pallas_call(functools.partial(states_body, layout, chunk), out_shape=l...]
    pallas_call x9 -> x10, Pallas kernels: 9.63 us -> 9.48 us  [run(): pl.pallas_call(functools.partial(work_body, self.layout, self.hops, intra...]
  transfers between devices with their start and end apart: 18 -> 20, of which waited for: 7 -> 8; matrix products, arithmetic and copies ran while one was open for 0% -> 0% of each run, Pallas kernels for 30% -> 31%
where the time goes in v3:
time: 47.2 us; the launch traced here: 46.8 us
  Pallas kernels  18 us (38%)
  starting transfers between devices  15.5 us (33%)
  waiting for transfers between devices  12.5 us (26%)
  between operations  0.52 us (1%)
    ppermute x11, starting transfers between devices, send(): received[hop, chunk] = lax.ppermute(value, 'seq', [(hop, hop + 1)])  10.7 us
    pallas_call x10, Pallas kernels, run(): pl.pallas_call(functools.partial(work_body, self.layout, self.hops, intra...  9.48 us
    ppermute x11, waiting for transfers between devices, send(): received[hop, chunk] = lax.ppermute(value, 'seq', [(hop, hop + 1)])  9.09 us
    pallas_call x1, Pallas kernels, load(): pl.pallas_call(functools.partial(load_body, layout, groups), out_shape=(j...  3.47 us
    ppermute x3, waiting for transfers between devices, sum_over_heads(): lax.ppermute(part, 'head', [(i, i ^ reach) for i in range(size)])  2.37 us
    ppermute x3, starting transfers between devices, sum_over_heads(): lax.ppermute(part, 'head', [(i, i ^ reach) for i in range(size)])  2.21 us
    pallas_call x1, Pallas kernels, finish(): pl.pallas_call(functools.partial(finish_body, heads, float(width)), out_s...  1.75 us
    pallas_call x4, Pallas kernels, states_of(): pl.pallas_call(functools.partial(states_body, layout, chunk), out_shape=l...  1.53 us
  transfers between devices with their start and end apart: 20, of which 8 were waited for; matrix products, arithmetic and copies ran while one was open for 0% of the time, Pallas kernels for 31%

profile of v3, /device:TPU:24, one launch (start us, length us, event | category | flops | bytes accessed | tf_op | source)
XLA Modules:
  0.0 46.8 jit_solution(6113291898741460108)
XLA Ops:
  0.0 1.5 %first.1.order_ref.state_ref = f32[328,128]{1,0:T(8,128)S(1)} custom-call(bf16[640,2048]{1,0:T(8,128)(2,1)} %k_hbm.3, bf16[640,2048]{1,0:T(8,128)(2,1)} %v_hbm.3), custom_call_target="tpu_custom_call" | custom-call | flops 1000 | bytes 1000 | tf_op jit(solution)/shard_map/first/pallas_call | solution.py:104
  1.5 0.1 collective-permute-start
  1.6 3.5 %load.1 = (bf16[640,2048]{1,0:T(8,128)(2,1)S(1)}, bf16[640,2048]{1,0:T(8,128)(2,1)S(1)}, bf16[640,2048]{1,0:T(8,128)(2,1)S(1)}, f32[344,128]{1,0:T(8,128)S(1)}) custom-call(bf16[640,2048]{1,0:T(8,128)(2,1)} %k_hbm.3, bf16[640,2048]{1,0:T(8,128)(2,1)} %v_hbm.3, bf16[640,2048]{1,0:T(8,128)(2,1)} %q_hbm.1, f32[328,128]{1,0:T(8,128)S(1)} %first.1.order_ref.state_ref), custom_call_target="tpu_custom_call" | custom-call | flops 1000 | bytes 1000 | tf_op jit(solution)/shard_map/load/pallas_call | solution.py:141
  5.1 0.6 %collective-permute-start.3 = (f32[344,128]{1,0:T(8,128)S(1)}, f32[344,128]{1,0:T(8,128)S(1)}, u32[]{:S(2)}, u32[]{:S(2)}) collective-permute-start(f32[344,128]{1,0:T(8,128)S(1)} %get-tuple-element.50.order_ref.state_ref), channel_id=1, source_target_pairs={{0,4},{1,5},{2,6},{3,7},{4,0},{5,1},{6,2},{7,3},{8,9},{9,8},{10,11... | collective-permute-start | bytes 528392 | tf_op jit(solution)/shard_map/ppermute | solution.py:390
  5.6 0.0 copy-start
  5.6 0.4 states.4.order_ref.state_ref
  6.0 0.1 collective-permute-start.2
  6.1 0.2 copy-done
  6.3 0.0 collective-permute-done.received_ref.refs_4_
  6.4 0.7 %collective-permute-start.1 = (f32[328,128]{1,0:T(8,128)S(1)}, f32[328,128]{1,0:T(8,128)S(1)}, u32[]{:S(2)}, u32[]{:S(2)}) collective-permute-start(f32[328,128]{1,0:T(8,128)S(1)} %merge.11.order_ref), channel_id=1, source_target_pairs={{4,8},{5,9},{6,10},{7,11},{20,24},{21,25},{22,26},{23,27}} | collective-permute-start | bytes 503816 | tf_op jit(solution)/shard_map/ppermute | solution.py:392
  7.0 0.4 states.5.refs_4_.state_ref
  7.5 0.3 collective-permute-start.8
  7.8 1.1 %work.10 = (f32[640,128]{1,0:T(8,128)S(1)}, f32[640,128]{1,0:T(8,128)S(1)}) custom-call(bf16[640,2048]{1,0:T(8,128)(2,1)S(1)} %get-tuple-element.47.refs_0_, bf16[640,2048]{1,0:T(8,128)(2,1)S(1)} %get-tuple-element.48.k_ref.refs_1_, bf16[640,2048]{1,0:T(8,128)(2,1)S(1)} %get-tuple-element.49.v_ref.refs_2_, bf16[1,2048]{1,0:T(2,128)(2,1)S(1)} %reshape.3.refs_3_, ...), custom_call_target="tpu_custom_call" | custom-call | flops 1600001024 | bytes 1000 | tf_op jit(solution)/shard_map/work/pallas_call | solution.py:288
  8.9 0.0 collective-permute-done.3.received_ref.refs_7_.refs_4_
  8.9 0.7 %collective-permute-start.7 = (f32[344,128]{1,0:T(8,128)S(1)}, f32[344,128]{1,0:T(8,128)S(1)}, u32[]{:S(2)}, u32[]{:S(2)}) collective-permute-start(f32[344,128]{1,0:T(8,128)S(1)} %merge.12.order_ref), channel_id=1, source_target_pairs={{4,8},{5,9},{6,10},{7,11},{20,24},{21,25},{22,26},{23,27}} | collective-permute-start | bytes 528392 | tf_op jit(solution)/shard_map/ppermute | solution.py:392
  9.6 0.4 states.6.refs_4_.state_ref
  10.0 1.1 %work.11 = (f32[640,128]{1,0:T(8,128)S(1)}, f32[640,128]{1,0:T(8,128)S(1)}) custom-call(bf16[640,2048]{1,0:T(8,128)(2,1)S(1)} %get-tuple-element.47.refs_0_, bf16[640,2048]{1,0:T(8,128)(2,1)S(1)} %get-tuple-element.48.k_ref.refs_1_, bf16[640,2048]{1,0:T(8,128)(2,1)S(1)} %get-tuple-element.49.v_ref.refs_2_, bf16[1,2048]{1,0:T(2,128)(2,1)S(1)} %reshape.3.refs_3_, ...), custom_call_target="tpu_custom_call" | custom-call | flops 1600001024 | bytes 1000 | tf_op jit(solution)/shard_map/work/pallas_call | solution.py:288
  11.0 0.3 collective-permute-start.6
  11.4 0.0 collective-permute-done.2.received_ref.refs_7_.refs_4_
  11.4 0.7 %collective-permute-start.5 = (f32[344,128]{1,0:T(8,128)S(1)}, f32[344,128]{1,0:T(8,128)S(1)}, u32[]{:S(2)}, u32[]{:S(2)}) collective-permute-start(f32[344,128]{1,0:T(8,128)S(1)} %merge.13.order_ref), channel_id=1, source_target_pairs={{4,8},{5,9},{6,10},{7,11},{20,24},{21,25},{22,26},{23,27}} | collective-permute-start | bytes 528392 | tf_op jit(solution)/shard_map/ppermute | solution.py:392
  12.1 0.4 states.7.late_ref.order_ref.state_ref
  12.4 0.0 collective-permute-done.1.received_ref.refs_5_
  12.5 1.3 %collective-permute-start.4 = (f32[344,128]{1,0:T(8,128)S(1)}, f32[344,128]{1,0:T(8,128)S(1)}, u32[]{:S(2)}, u32[]{:S(2)}) collective-permute-start(f32[344,128]{1,0:T(8,128)S(1)} %merge_two.1.refs_4_), channel_id=1, source_target_pairs={{0,4},{8,12},{1,5},{9,13},{2,6},{10,14},{3,7},{11,15},{16,20},{24,... | collective-permute-start | bytes 528392 | tf_op jit(solution)/shard_map/ppermute | solution.py:420
  13.8 1.1 %work.12 = (f32[640,128]{1,0:T(8,128)S(1)}, f32[640,128]{1,0:T(8,128)S(1)}) custom-call(bf16[640,2048]{1,0:T(8,128)(2,1)S(1)} %get-tuple-element.47.refs_0_, bf16[640,2048]{1,0:T(8,128)(2,1)S(1)} %get-tuple-element.48.k_ref.refs_1_, bf16[640,2048]{1,0:T(8,128)(2,1)S(1)} %get-tuple-element.49.v_ref.refs_2_, bf16[1,2048]{1,0:T(2,128)(2,1)S(1)} %reshape.3.refs_3_, ...), custom_call_target="tpu_custom_call" | custom-call | flops 1600001024 | bytes 1000 | tf_op jit(solution)/shard_map/work/pallas_call | solution.py:288
  14.8 0.0 collective-permute-done.8.received_ref.refs_7_.refs_4_
  14.9 0.7 %collective-permute-start.10 = (f32[344,128]{1,0:T(8,128)S(1)}, f32[344,128]{1,0:T(8,128)S(1)}, u32[]{:S(2)}, u32[]{:S(2)}) collective-permute-start(f32[344,128]{1,0:T(8,128)S(1)} %merge.14.order_ref), channel_id=1, source_target_pairs={{4,8},{5,9},{6,10},{7,11},{20,24},{21,25},{22,26},{23,27}} | collective-permute-start | bytes 528392 | tf_op jit(solution)/shard_map/ppermute | solution.py:392
  15.6 0.0 collective-permute-done.7.received_ref.refs_8_.refs_5_
  15.6 1.3 %collective-permute-start.9 = (f32[344,128]{1,0:T(8,128)S(1)}, f32[344,128]{1,0:T(8,128)S(1)}, u32[]{:S(2)}, u32[]{:S(2)}) collective-permute-start(f32[344,128]{1,0:T(8,128)S(1)} %merge.15.refs_4_), channel_id=1, source_target_pairs={{8,12},{9,13},{10,14},{11,15},{24,28},{25,29},{26,30},{27,31}} | collective-permute-start | bytes 528392 | tf_op jit(solution)/shard_map/ppermute | solution.py:392
  16.9 1.1 %work.13 = (f32[640,128]{1,0:T(8,128)S(1)}, f32[640,128]{1,0:T(8,128)S(1)}) custom-call(bf16[640,2048]{1,0:T(8,128)(2,1)S(1)} %get-tuple-element.47.refs_0_, bf16[640,2048]{1,0:T(8,128)(2,1)S(1)} %get-tuple-element.48.k_ref.refs_1_, bf16[640,2048]{1,0:T(8,128)(2,1)S(1)} %get-tuple-element.49.v_ref.refs_2_, bf16[1,2048]{1,0:T(2,128)(2,1)S(1)} %reshape.3.refs_3_, ...), custom_call_target="tpu_custom_call" | custom-call | flops 1600001024 | bytes 1000 | tf_op jit(solution)/shard_map/work/pallas_call | solution.py:288
  18.0 0.0 collective-permute-done.6.received_ref.refs_7_.refs_4_
  18.0 0.7 %collective-permute-start.12 = (f32[344,128]{1,0:T(8,128)S(1)}, f32[344,128]{1,0:T(8,128)S(1)}, u32[]{:S(2)}, u32[]{:S(2)}) collective-permute-start(f32[344,128]{1,0:T(8,128)S(1)} %merge.16.order_ref), channel_id=1, source_target_pairs={{4,8},{5,9},{6,10},{7,11},{20,24},{21,25},{22,26},{23,27}} | collective-permute-start | bytes 528392 | tf_op jit(solution)/shard_map/ppermute | solution.py:392
  18.7 0.0 collective-permute-done.5.received_ref.refs_8_.refs_5_
  18.7 1.3 %collective-permute-start.11 = (f32[344,128]{1,0:T(8,128)S(1)}, f32[344,128]{1,0:T(8,128)S(1)}, u32[]{:S(2)}, u32[]{:S(2)}) collective-permute-start(f32[344,128]{1,0:T(8,128)S(1)} %merge.17.refs_9_), channel_id=1, source_target_pairs={{8,12},{9,13},{10,14},{11,15},{24,28},{25,29},{26,30},{27,31}} | collective-permute-start | bytes 528392 | tf_op jit(solution)/shard_map/ppermute | solution.py:392
  20.0 1.0 %collective-permute-done.4.refs_6_.received_ref.refs_7_ = f32[344,128]{1,0:T(8,128)S(1)} collective-permute-done((f32[344,128]{1,0:T(8,128)S(1)}, f32[344,128]{1,0:T(8,128)S(1)}, u32[]{:S(2)}, u32[]{:S(2)}) %collective-permute-start.4) | collective-permute-done | bytes 176160 | tf_op jit(solution)/shard_map/ppermute | solution.py:420
  21.0 1.1 %work.14 = (f32[640,128]{1,0:T(8,128)S(1)}, f32[640,128]{1,0:T(8,128)S(1)}, f32[640,128]{1,0:T(8,128)S(1)}, f32[640,128]{1,0:T(8,128)S(1)}, f32[640,128]{1,0:T(8,128)S(1)}) custom-call(bf16[640,2048]{1,0:T(8,128)(2,1)S(1)} %get-tuple-element.47.refs_0_, bf16[640,2048]{1,0:T(8,128)(2,1)S(1)} %get-tuple-element.48.k_ref.refs_1_, ...), custom_call_target="tpu_custom_call" | custom-call | flops 2000001024 | bytes 1000 | tf_op jit(solution)/shard_map/work/pallas_call | solution.py:288
  22.1 0.7 %collective-permute-start.14 = (f32[344,128]{1,0:T(8,128)S(1)}, f32[344,128]{1,0:T(8,128)S(1)}, u32[]{:S(2)}, u32[]{:S(2)}) collective-permute-start(f32[344,128]{1,0:T(8,128)S(1)} %merge.18.order_ref), channel_id=1, source_target_pairs={{4,8},{5,9},{6,10},{7,11},{20,24},{21,25},{22,26},{23,27}} | collective-permute-start | bytes 528392 | tf_op jit(solution)/shard_map/ppermute | solution.py:392
  22.8 0.0 collective-permute-done.10.received_ref.refs_8_.refs_5_
  22.9 1.3 %collective-permute-start.13 = (f32[344,128]{1,0:T(8,128)S(1)}, f32[344,128]{1,0:T(8,128)S(1)}, u32[]{:S(2)}, u32[]{:S(2)}) collective-permute-start(f32[344,128]{1,0:T(8,128)S(1)} %merge.19.refs_14_), channel_id=1, source_target_pairs={{8,12},{9,13},{10,14},{11,15},{24,28},{25,29},{26,30},{27,31}} | collective-permute-start | bytes 528392 | tf_op jit(solution)/shard_map/ppermute | solution.py:392
  24.2 0.6 %collective-permute-done.9.refs_9_.refs_6_ = f32[344,128]{1,0:T(8,128)S(1)} collective-permute-done((f32[344,128]{1,0:T(8,128)S(1)}, f32[344,128]{1,0:T(8,128)S(1)}, u32[]{:S(2)}, u32[]{:S(2)}) %collective-permute-start.9) | collective-permute-done | bytes 176160 | tf_op jit(solution)/shard_map/ppermute | solution.py:392
  24.8 1.1 %work.15 = (f32[640,128]{1,0:T(8,128)S(1)}, f32[640,128]{1,0:T(8,128)S(1)}, f32[640,128]{1,0:T(8,128)S(1)}, f32[640,128]{1,0:T(8,128)S(1)}, f32[640,128]{1,0:T(8,128)S(1)}, /*index=5*/f32[640,128]{1,0:T(8,128)S(1)}) custom-call(bf16[640,2048]{1,0:T(8,128)(2,1)S(1)} %get-tuple-element.47.refs_0_, bf16[640,2048]{1,0:T(8,128)(2,1)S(1)} %get-tuple-element.48.k_ref.refs_1_, ...), custom_call_target="tpu_custom_call" | custom-call | flops 2200001024 | bytes 1000 | tf_op jit(solution)/shard_map/work/pallas_call | solution.py:288
  25.9 0.0 collective-permute-done.12.received_ref.refs_8_.refs_5_
  26.0 1.3 %collective-permute-start.15 = (f32[344,128]{1,0:T(8,128)S(1)}, f32[344,128]{1,0:T(8,128)S(1)}, u32[]{:S(2)}, u32[]{:S(2)}) collective-permute-start(f32[344,128]{1,0:T(8,128)S(1)} %merge.20.refs_13_), channel_id=1, source_target_pairs={{8,12},{9,13},{10,14},{11,15},{24,28},{25,29},{26,30},{27,31}} | collective-permute-start | bytes 528392 | tf_op jit(solution)/shard_map/ppermute | solution.py:392
  27.3 1.3 %collective-permute-done.11.refs_9_.refs_6_ = f32[344,128]{1,0:T(8,128)S(1)} collective-permute-done((f32[344,128]{1,0:T(8,128)S(1)}, f32[344,128]{1,0:T(8,128)S(1)}, u32[]{:S(2)}, u32[]{:S(2)}) %collective-permute-start.11) | collective-permute-done | bytes 176160 | tf_op jit(solution)/shard_map/ppermute | solution.py:392
  28.6 1.1 %work.16 = (f32[640,128]{1,0:T(8,128)S(1)}, f32[640,128]{1,0:T(8,128)S(1)}, f32[640,128]{1,0:T(8,128)S(1)}, f32[640,128]{1,0:T(8,128)S(1)}, f32[640,128]{1,0:T(8,128)S(1)}) custom-call(bf16[640,2048]{1,0:T(8,128)(2,1)S(1)} %get-tuple-element.47.refs_0_, bf16[640,2048]{1,0:T(8,128)(2,1)S(1)} %get-tuple-element.48.k_ref.refs_1_, ...), custom_call_target="tpu_custom_call" | custom-call | flops 2000001024 | bytes 1000 | tf_op jit(solution)/shard_map/work/pallas_call | solution.py:288
  29.7 0.0 collective-permute-done.14.received_ref.refs_8_
  29.7 1.5 %collective-permute-start.16 = (f32[344,128]{1,0:T(8,128)S(1)}, f32[344,128]{1,0:T(8,128)S(1)}, u32[]{:S(2)}, u32[]{:S(2)}) collective-permute-start(f32[344,128]{1,0:T(8,128)S(1)} %merge.21.refs_14_), channel_id=1, source_target_pairs={{8,12},{9,13},{10,14},{11,15},{24,28},{25,29},{26,30},{27,31}} | collective-permute-start | bytes 528392 | tf_op jit(solution)/shard_map/ppermute | solution.py:392
  31.2 2.2 %collective-permute-done.13.refs_9_.refs_6_ = f32[344,128]{1,0:T(8,128)S(1)} collective-permute-done((f32[344,128]{1,0:T(8,128)S(1)}, f32[344,128]{1,0:T(8,128)S(1)}, u32[]{:S(2)}, u32[]{:S(2)}) %collective-permute-start.13) | collective-permute-done | bytes 176160 | tf_op jit(solution)/shard_map/ppermute | solution.py:392
  33.4 1.2 %work.17 = (f32[640,128]{1,0:T(8,128)S(1)}, f32[640,128]{1,0:T(8,128)S(1)}, f32[640,128]{1,0:T(8,128)S(1)}, f32[640,128]{1,0:T(8,128)S(1)}, f32[640,128]{1,0:T(8,128)S(1)}, /*index=5*/f32[640,128]{1,0:T(8,128)S(1)}) custom-call(bf16[640,2048]{1,0:T(8,128)(2,1)S(1)} %get-tuple-element.47.refs_0_, bf16[640,2048]{1,0:T(8,128)(2,1)S(1)} %get-tuple-element.48.k_ref.refs_1_, ...), custom_call_target="tpu_custom_call" | custom-call | flops 2200001024 | bytes 1000 | tf_op jit(solution)/shard_map/work/pallas_call | solution.py:288
  34.5 2.4 %collective-permute-done.15.refs_9_.refs_6_ = f32[344,128]{1,0:T(8,128)S(1)} collective-permute-done((f32[344,128]{1,0:T(8,128)S(1)}, f32[344,128]{1,0:T(8,128)S(1)}, u32[]{:S(2)}, u32[]{:S(2)}) %collective-permute-start.15) | collective-permute-done | bytes 176160 | tf_op jit(solution)/shard_map/ppermute | solution.py:392
  36.9 0.3 work.18
  37.2 2.6 %collective-permute-done.16.refs_9_ = f32[344,128]{1,0:T(8,128)S(1)} collective-permute-done((f32[344,128]{1,0:T(8,128)S(1)}, f32[344,128]{1,0:T(8,128)S(1)}, u32[]{:S(2)}, u32[]{:S(2)}) %collective-permute-start.16) | collective-permute-done | bytes 176160 | tf_op jit(solution)/shard_map/ppermute | solution.py:392
  39.9 0.4 work.19
  40.3 1.6 %collective-permute-start.18 = (f32[1,640]{1,0:T(1,128)S(1)}, f32[1,640]{1,0:T(1,128)S(1)}, u32[]{:S(2)}, u32[]{:S(2)}) collective-permute-start(f32[1,640]{1,0:T(1,128)S(1)} %get-tuple-element.88), channel_id=1, source_target_pairs={{0,2},{1,3},{2,0},{3,1},{4,6},{5,7},{6,4},{7,5},{8,10},{9,11},{10,... | collective-permute-start | bytes 7688 | tf_op jit(solution)/shard_map/ppermute | solution.py:358
  41.9 0.0 collective-permute-start.19
  41.9 0.6 %collective-permute-start.17 = (f32[1,640]{1,0:T(1,128)S(1)}, f32[1,640]{1,0:T(1,128)S(1)}, u32[]{:S(2)}, u32[]{:S(2)}) collective-permute-start(f32[1,640]{1,0:T(1,128)S(1)} %get-tuple-element.88), channel_id=1, source_target_pairs={{0,1},{1,0},{2,3},{3,2},{4,5},{5,4},{6,7},{7,6},{8,9},{9,8},{10,11... | collective-permute-start | bytes 7688 | tf_op jit(solution)/shard_map/ppermute | solution.py:358
  42.5 1.4 %collective-permute-done.18 = f32[1,640]{1,0:T(1,128)S(1)} collective-permute-done((f32[1,640]{1,0:T(1,128)S(1)}, f32[1,640]{1,0:T(1,128)S(1)}, u32[]{:S(2)}, u32[]{:S(2)}) %collective-permute-start.18) | collective-permute-done | bytes 2592 | tf_op jit(solution)/shard_map/ppermute | solution.py:358
  43.9 0.9 %collective-permute-done.19 = f32[1,640]{1,0:T(1,128)S(1)} collective-permute-done((f32[1,640]{1,0:T(1,128)S(1)}, f32[1,640]{1,0:T(1,128)S(1)}, u32[]{:S(2)}, u32[]{:S(2)}) %collective-permute-start.19) | collective-permute-done | bytes 2592 | tf_op jit(solution)/shard_map/ppermute | solution.py:358
  44.9 0.0 collective-permute-done.17
  44.9 1.8 %finish.1 = bf16[640,2048]{1,0:T(8,128)(2,1)} custom-call(f32[640,128]{1,0:T(8,128)S(1)} %get-tuple-element.56.refs_0_, f32[640,128]{1,0:T(8,128)S(1)} %get-tuple-element.57.refs_1_, f32[640,128]{1,0:T(8,128)S(1)} %get-tuple-element.62.refs_2_, f32[640,128]{1,0:T(8,128)S(1)} %get-tuple-element.63.refs_3_, f32[640,128]{1,0:T(8,128)S(1)} %get-tuple-element.64.refs_4_, ...), custom_call_target="tpu_custom_call" | custom-call | tf_op jit(solution)/shard_map/finish/pallas_call | solution.py:339
  (14 shorter events, 0.3 us)
Async XLA Ops:
  1.5 4.8 %collective-permute-start = (f32[328,128]{1,0:T(8,128)S(1)}, f32[328,128]{1,0:T(8,128)S(1)}, u32[]{:S(2)}, u32[]{:S(2)}) collective-permute-start(f32[328,128]{1,0:T(8,128)S(1)} %first.1.order_ref.state_ref), channel_id=1, source_target_pairs={{0,4},{1,5},{2,6},{3,7},{4,0},{5,1},{6,2},{7,3},{8,9},{9,8},{10,11... | collective-permute-start | bytes 503816 | tf_op jit(solution)/shard_map/ppermute | solution.py:390
  5.1 3.8 %collective-permute-start.3 = (f32[344,128]{1,0:T(8,128)S(1)}, f32[344,128]{1,0:T(8,128)S(1)}, u32[]{:S(2)}, u32[]{:S(2)}) collective-permute-start(f32[344,128]{1,0:T(8,128)S(1)} %get-tuple-element.50.order_ref.state_ref), channel_id=1, source_target_pairs={{0,4},{1,5},{2,6},{3,7},{4,0},{5,1},{6,2},{7,3},{8,9},{9,8},{10,11... | collective-permute-start | bytes 528392 | tf_op jit(solution)/shard_map/ppermute | solution.py:390
  5.6 0.7 %copy-start = (bf16[2048]{0:T(1024)(128)(2,1)S(1)}, bf16[2048]{0:T(1024)(128)(2,1)}, u32[]{:S(2)}) copy-start(bf16[2048]{0:T(1024)(128)(2,1)} %param.7) | copy-start | bytes 12292
  6.0 5.3 %collective-permute-start.2 = (f32[344,128]{1,0:T(8,128)S(1)}, f32[344,128]{1,0:T(8,128)S(1)}, u32[]{:S(2)}, u32[]{:S(2)}) collective-permute-start(f32[344,128]{1,0:T(8,128)S(1)} %states.4.order_ref.state_ref), channel_id=1, source_target_pairs={{0,4},{1,5},{2,6},{3,7},{4,0},{5,1},{6,2},{7,3},{8,9},{9,8},{10,11... | collective-permute-start | bytes 528392 | tf_op jit(solution)/shard_map/ppermute | solution.py:390
  6.4 6.1 %collective-permute-start.1 = (f32[328,128]{1,0:T(8,128)S(1)}, f32[328,128]{1,0:T(8,128)S(1)}, u32[]{:S(2)}, u32[]{:S(2)}) collective-permute-start(f32[328,128]{1,0:T(8,128)S(1)} %merge.11.order_ref), channel_id=1, source_target_pairs={{4,8},{5,9},{6,10},{7,11},{20,24},{21,25},{22,26},{23,27}} | collective-permute-start | bytes 503816 | tf_op jit(solution)/shard_map/ppermute | solution.py:392
  7.5 7.4 %collective-permute-start.8 = (f32[344,128]{1,0:T(8,128)S(1)}, f32[344,128]{1,0:T(8,128)S(1)}, u32[]{:S(2)}, u32[]{:S(2)}) collective-permute-start(f32[344,128]{1,0:T(8,128)S(1)} %states.5.refs_4_.state_ref), channel_id=1, source_target_pairs={{0,4},{1,5},{2,6},{3,7},{4,0},{5,1},{6,2},{7,3},{8,9},{9,8},{10,11... | collective-permute-start | bytes 528392 | tf_op jit(solution)/shard_map/ppermute | solution.py:390
  8.9 6.7 %collective-permute-start.7 = (f32[344,128]{1,0:T(8,128)S(1)}, f32[344,128]{1,0:T(8,128)S(1)}, u32[]{:S(2)}, u32[]{:S(2)}) collective-permute-start(f32[344,128]{1,0:T(8,128)S(1)} %merge.12.order_ref), channel_id=1, source_target_pairs={{4,8},{5,9},{6,10},{7,11},{20,24},{21,25},{22,26},{23,27}} | collective-permute-start | bytes 528392 | tf_op jit(solution)/shard_map/ppermute | solution.py:392
  11.0 6.9 %collective-permute-start.6 = (f32[344,128]{1,0:T(8,128)S(1)}, f32[344,128]{1,0:T(8,128)S(1)}, u32[]{:S(2)}, u32[]{:S(2)}) collective-permute-start(f32[344,128]{1,0:T(8,128)S(1)} %states.6.refs_4_.state_ref), channel_id=1, source_target_pairs={{0,4},{1,5},{2,6},{3,7},{4,0},{5,1},{6,2},{7,3},{8,9},{9,8},{10,11... | collective-permute-start | bytes 528392 | tf_op jit(solution)/shard_map/ppermute | solution.py:390
  11.4 7.3 %collective-permute-start.5 = (f32[344,128]{1,0:T(8,128)S(1)}, f32[344,128]{1,0:T(8,128)S(1)}, u32[]{:S(2)}, u32[]{:S(2)}) collective-permute-start(f32[344,128]{1,0:T(8,128)S(1)} %merge.13.order_ref), channel_id=1, source_target_pairs={{4,8},{5,9},{6,10},{7,11},{20,24},{21,25},{22,26},{23,27}} | collective-permute-start | bytes 528392 | tf_op jit(solution)/shard_map/ppermute | solution.py:392
  12.5 8.5 %collective-permute-start.4 = (f32[344,128]{1,0:T(8,128)S(1)}, f32[344,128]{1,0:T(8,128)S(1)}, u32[]{:S(2)}, u32[]{:S(2)}) collective-permute-start(f32[344,128]{1,0:T(8,128)S(1)} %merge_two.1.refs_4_), channel_id=1, source_target_pairs={{0,4},{8,12},{1,5},{9,13},{2,6},{10,14},{3,7},{11,15},{16,20},{24,... | collective-permute-start | bytes 528392 | tf_op jit(solution)/shard_map/ppermute | solution.py:420
  14.9 7.9 %collective-permute-start.10 = (f32[344,128]{1,0:T(8,128)S(1)}, f32[344,128]{1,0:T(8,128)S(1)}, u32[]{:S(2)}, u32[]{:S(2)}) collective-permute-start(f32[344,128]{1,0:T(8,128)S(1)} %merge.14.order_ref), channel_id=1, source_target_pairs={{4,8},{5,9},{6,10},{7,11},{20,24},{21,25},{22,26},{23,27}} | collective-permute-start | bytes 528392 | tf_op jit(solution)/shard_map/ppermute | solution.py:392
  15.6 9.2 %collective-permute-start.9 = (f32[344,128]{1,0:T(8,128)S(1)}, f32[344,128]{1,0:T(8,128)S(1)}, u32[]{:S(2)}, u32[]{:S(2)}) collective-permute-start(f32[344,128]{1,0:T(8,128)S(1)} %merge.15.refs_4_), channel_id=1, source_target_pairs={{8,12},{9,13},{10,14},{11,15},{24,28},{25,29},{26,30},{27,31}} | collective-permute-start | bytes 528392 | tf_op jit(solution)/shard_map/ppermute | solution.py:392
  18.0 7.9 %collective-permute-start.12 = (f32[344,128]{1,0:T(8,128)S(1)}, f32[344,128]{1,0:T(8,128)S(1)}, u32[]{:S(2)}, u32[]{:S(2)}) collective-permute-start(f32[344,128]{1,0:T(8,128)S(1)} %merge.16.order_ref), channel_id=1, source_target_pairs={{4,8},{5,9},{6,10},{7,11},{20,24},{21,25},{22,26},{23,27}} | collective-permute-start | bytes 528392 | tf_op jit(solution)/shard_map/ppermute | solution.py:392
  18.7 9.8 %collective-permute-start.11 = (f32[344,128]{1,0:T(8,128)S(1)}, f32[344,128]{1,0:T(8,128)S(1)}, u32[]{:S(2)}, u32[]{:S(2)}) collective-permute-start(f32[344,128]{1,0:T(8,128)S(1)} %merge.17.refs_9_), channel_id=1, source_target_pairs={{8,12},{9,13},{10,14},{11,15},{24,28},{25,29},{26,30},{27,31}} | collective-permute-start | bytes 528392 | tf_op jit(solution)/shard_map/ppermute | solution.py:392
  22.1 7.5 %collective-permute-start.14 = (f32[344,128]{1,0:T(8,128)S(1)}, f32[344,128]{1,0:T(8,128)S(1)}, u32[]{:S(2)}, u32[]{:S(2)}) collective-permute-start(f32[344,128]{1,0:T(8,128)S(1)} %merge.18.order_ref), channel_id=1, source_target_pairs={{4,8},{5,9},{6,10},{7,11},{20,24},{21,25},{22,26},{23,27}} | collective-permute-start | bytes 528392 | tf_op jit(solution)/shard_map/ppermute | solution.py:392
  22.9 10.5 %collective-permute-start.13 = (f32[344,128]{1,0:T(8,128)S(1)}, f32[344,128]{1,0:T(8,128)S(1)}, u32[]{:S(2)}, u32[]{:S(2)}) collective-permute-start(f32[344,128]{1,0:T(8,128)S(1)} %merge.19.refs_14_), channel_id=1, source_target_pairs={{8,12},{9,13},{10,14},{11,15},{24,28},{25,29},{26,30},{27,31}} | collective-permute-start | bytes 528392 | tf_op jit(solution)/shard_map/ppermute | solution.py:392
  26.0 10.9 %collective-permute-start.15 = (f32[344,128]{1,0:T(8,128)S(1)}, f32[344,128]{1,0:T(8,128)S(1)}, u32[]{:S(2)}, u32[]{:S(2)}) collective-permute-start(f32[344,128]{1,0:T(8,128)S(1)} %merge.20.refs_13_), channel_id=1, source_target_pairs={{8,12},{9,13},{10,14},{11,15},{24,28},{25,29},{26,30},{27,31}} | collective-permute-start | bytes 528392 | tf_op jit(solution)/shard_map/ppermute | solution.py:392
  29.7 10.2 %collective-permute-start.16 = (f32[344,128]{1,0:T(8,128)S(1)}, f32[344,128]{1,0:T(8,128)S(1)}, u32[]{:S(2)}, u32[]{:S(2)}) collective-permute-start(f32[344,128]{1,0:T(8,128)S(1)} %merge.21.refs_14_), channel_id=1, source_target_pairs={{8,12},{9,13},{10,14},{11,15},{24,28},{25,29},{26,30},{27,31}} | collective-permute-start | bytes 528392 | tf_op jit(solution)/shard_map/ppermute | solution.py:392
  40.3 3.7 %collective-permute-start.18 = (f32[1,640]{1,0:T(1,128)S(1)}, f32[1,640]{1,0:T(1,128)S(1)}, u32[]{:S(2)}, u32[]{:S(2)}) collective-permute-start(f32[1,640]{1,0:T(1,128)S(1)} %get-tuple-element.88), channel_id=1, source_target_pairs={{0,2},{1,3},{2,0},{3,1},{4,6},{5,7},{6,4},{7,5},{8,10},{9,11},{10,... | collective-permute-start | bytes 7688 | tf_op jit(solution)/shard_map/ppermute | solution.py:358
  41.9 3.0 %collective-permute-start.19 = (f32[1,640]{1,0:T(1,128)S(1)}, f32[1,640]{1,0:T(1,128)S(1)}, u32[]{:S(2)}, u32[]{:S(2)}) collective-permute-start(f32[1,640]{1,0:T(1,128)S(1)} %get-tuple-element.88), channel_id=1, source_target_pairs={{0,3},{1,2},{2,1},{3,0},{4,7},{5,6},{6,5},{7,4},{8,11},{9,10},{10,... | collective-permute-start | bytes 7688 | tf_op jit(solution)/shard_map/ppermute | solution.py:358
  41.9 3.0 %collective-permute-start.17 = (f32[1,640]{1,0:T(1,128)S(1)}, f32[1,640]{1,0:T(1,128)S(1)}, u32[]{:S(2)}, u32[]{:S(2)}) collective-permute-start(f32[1,640]{1,0:T(1,128)S(1)} %get-tuple-element.88), channel_id=1, source_target_pairs={{0,1},{1,0},{2,3},{3,2},{4,5},{5,4},{6,7},{7,6},{8,9},{9,8},{10,11... | collective-permute-start | bytes 7688 | tf_op jit(solution)/shard_map/ppermute | solution.py:358

commit v4 on v3

--- a/solution.py
+++ b/solution.py
@@ -423,7 +423,8 @@
                 send(hop, c, worker.token)
         if wave + AHEAD < min(own, chunks):
             send_own(wave + AHEAD)
-        quota = -(-len(left) // max(1, INTRA - wave))
+        rest = max(1, INTRA - wave - (1 if wave < own - 1 else 0))
+        quota = 0 if wave == own - 1 else -(-len(left) // rest)
         intra, left = left[:quota], left[quota:]
         inter = []
         c = wave - TRAIL * max(0, hops - 2) - 2

time: 47.2 us -> 47.9 us (1.015)
  waiting for transfers between devices: 12.5 us -> 13.3 us
    ppermute x11, waiting for transfers between devices: 9.09 us -> 9.94 us  [send(): received[hop, chunk] = lax.ppermute(value, 'seq', [(hop, hop + 1)])]
  transfers between devices with their start and end apart: 20 -> 20, of which waited for: 8 -> 8; matrix products, arithmetic and copies ran while one was open for 0% -> 0% of each run, Pallas kernels for 31% -> 30%
where the time goes in v4:
time: 47.9 us; the launch traced here: 47.6 us
  Pallas kernels  18 us (38%)
  starting transfers between devices  15.5 us (32%)
  waiting for transfers between devices  13.3 us (28%)
  between operations  0.51 us (1%)
    ppermute x11, starting transfers between devices, send(): received[hop, chunk] = lax.ppermute(value, 'seq', [(hop, hop + 1)])  10.7 us
    ppermute x11, waiting for transfers between devices, send(): received[hop, chunk] = lax.ppermute(value, 'seq', [(hop, hop + 1)])  9.94 us
    pallas_call x10, Pallas kernels, run(): pl.pallas_call(functools.partial(work_body, self.layout, self.hops, intra...  9.42 us
    pallas_call x1, Pallas kernels, load(): pl.pallas_call(functools.partial(load_body, layout, groups), out_shape=(j...  3.47 us
    ppermute x3, waiting for transfers between devices, sum_over_heads(): lax.ppermute(part, 'head', [(i, i ^ reach) for i in range(size)])  2.37 us
    ppermute x3, starting transfers between devices, sum_over_heads(): lax.ppermute(part, 'head', [(i, i ^ reach) for i in range(size)])  2.21 us
    pallas_call x1, Pallas kernels, finish(): pl.pallas_call(functools.partial(finish_body, heads, float(width)), out_s...  1.74 us
    pallas_call x4, Pallas kernels, states_of(): pl.pallas_call(functools.partial(states_body, layout, chunk), out_shape=l...  1.53 us
  transfers between devices with their start and end apart: 20, of which 8 were waited for; matrix products, arithmetic and copies ran while one was open for 0% of the time, Pallas kernels for 30%

profile of v4, /device:TPU:24, one launch (start us, length us, event | category | flops | bytes accessed | tf_op | source)
XLA Modules:
  0.0 47.6 jit_solution(17513038648459175219)
XLA Ops:
  0.0 1.5 %first.1.order_ref.state_ref = f32[328,128]{1,0:T(8,128)S(1)} custom-call(bf16[640,2048]{1,0:T(8,128)(2,1)} %k_hbm.3, bf16[640,2048]{1,0:T(8,128)(2,1)} %v_hbm.3), custom_call_target="tpu_custom_call" | custom-call | flops 1000 | bytes 1000 | tf_op jit(solution)/shard_map/first/pallas_call | solution.py:104
  1.5 0.1 collective-permute-start
  1.6 3.5 %load.1 = (bf16[640,2048]{1,0:T(8,128)(2,1)S(1)}, bf16[640,2048]{1,0:T(8,128)(2,1)S(1)}, bf16[640,2048]{1,0:T(8,128)(2,1)S(1)}, f32[344,128]{1,0:T(8,128)S(1)}) custom-call(bf16[640,2048]{1,0:T(8,128)(2,1)} %k_hbm.3, bf16[640,2048]{1,0:T(8,128)(2,1)} %v_hbm.3, bf16[640,2048]{1,0:T(8,128)(2,1)} %q_hbm.1, f32[328,128]{1,0:T(8,128)S(1)} %first.1.order_ref.state_ref), custom_call_target="tpu_custom_call" | custom-call | flops 1000 | bytes 1000 | tf_op jit(solution)/shard_map/load/pallas_call | solution.py:141
  5.1 0.6 %collective-permute-start.3 = (f32[344,128]{1,0:T(8,128)S(1)}, f32[344,128]{1,0:T(8,128)S(1)}, u32[]{:S(2)}, u32[]{:S(2)}) collective-permute-start(f32[344,128]{1,0:T(8,128)S(1)} %get-tuple-element.50.order_ref.state_ref), channel_id=1, source_target_pairs={{0,4},{1,5},{2,6},{3,7},{4,0},{5,1},{6,2},{7,3},{8,9},{9,8},{10,11... | collective-permute-start | bytes 528392 | tf_op jit(solution)/shard_map/ppermute | solution.py:390
  5.6 0.0 copy-start
  5.6 0.4 states.4.order_ref.state_ref
  6.0 0.1 collective-permute-start.2
  6.1 0.2 copy-done
  6.3 0.0 collective-permute-done.received_ref.refs_4_
  6.4 0.7 %collective-permute-start.1 = (f32[328,128]{1,0:T(8,128)S(1)}, f32[328,128]{1,0:T(8,128)S(1)}, u32[]{:S(2)}, u32[]{:S(2)}) collective-permute-start(f32[328,128]{1,0:T(8,128)S(1)} %merge.11.order_ref), channel_id=1, source_target_pairs={{4,8},{5,9},{6,10},{7,11},{20,24},{21,25},{22,26},{23,27}} | collective-permute-start | bytes 503816 | tf_op jit(solution)/shard_map/ppermute | solution.py:392
  7.0 0.4 states.5.refs_4_.state_ref
  7.5 0.3 collective-permute-start.8
  7.8 1.4 %work.10 = (f32[640,128]{1,0:T(8,128)S(1)}, f32[640,128]{1,0:T(8,128)S(1)}, f32[640,128]{1,0:T(8,128)S(1)}) custom-call(bf16[640,2048]{1,0:T(8,128)(2,1)S(1)} %get-tuple-element.47.refs_0_, bf16[640,2048]{1,0:T(8,128)(2,1)S(1)} %get-tuple-element.48.k_ref.refs_1_, bf16[640,2048]{1,0:T(8,128)(2,1)S(1)} %get-tuple-element.49.v_ref.refs_2_, ...), custom_call_target="tpu_custom_call" | custom-call | flops 2400001024 | bytes 1000 | tf_op jit(solution)/shard_map/work/pallas_call | solution.py:288
  9.2 0.0 collective-permute-done.3.received_ref.refs_7_.refs_4_
  9.3 0.4 states.6.refs_4_.state_ref
  9.7 0.7 %collective-permute-start.7 = (f32[344,128]{1,0:T(8,128)S(1)}, f32[344,128]{1,0:T(8,128)S(1)}, u32[]{:S(2)}, u32[]{:S(2)}) collective-permute-start(f32[344,128]{1,0:T(8,128)S(1)} %merge.12.order_ref), channel_id=1, source_target_pairs={{4,8},{5,9},{6,10},{7,11},{20,24},{21,25},{22,26},{23,27}} | collective-permute-start | bytes 528392 | tf_op jit(solution)/shard_map/ppermute | solution.py:392
  10.4 1.5 %work.11 = (f32[640,128]{1,0:T(8,128)S(1)}, f32[640,128]{1,0:T(8,128)S(1)}, f32[640,128]{1,0:T(8,128)S(1)}) custom-call(bf16[640,2048]{1,0:T(8,128)(2,1)S(1)} %get-tuple-element.47.refs_0_, bf16[640,2048]{1,0:T(8,128)(2,1)S(1)} %get-tuple-element.48.k_ref.refs_1_, bf16[640,2048]{1,0:T(8,128)(2,1)S(1)} %get-tuple-element.49.v_ref.refs_2_, ...), custom_call_target="tpu_custom_call" | custom-call | flops 2400001024 | bytes 1000 | tf_op jit(solution)/shard_map/work/pallas_call | solution.py:288
  11.8 0.3 collective-permute-start.6
  12.1 0.0 collective-permute-done.2.received_ref.refs_7_.refs_4_
  12.2 0.7 %collective-permute-start.5 = (f32[344,128]{1,0:T(8,128)S(1)}, f32[344,128]{1,0:T(8,128)S(1)}, u32[]{:S(2)}, u32[]{:S(2)}) collective-permute-start(f32[344,128]{1,0:T(8,128)S(1)} %merge.13.order_ref), channel_id=1, source_target_pairs={{4,8},{5,9},{6,10},{7,11},{20,24},{21,25},{22,26},{23,27}} | collective-permute-start | bytes 528392 | tf_op jit(solution)/shard_map/ppermute | solution.py:392
  12.9 0.4 states.7.late_ref.order_ref.state_ref
  13.2 0.0 collective-permute-done.1.received_ref.refs_5_
  13.3 1.3 %collective-permute-start.4 = (f32[344,128]{1,0:T(8,128)S(1)}, f32[344,128]{1,0:T(8,128)S(1)}, u32[]{:S(2)}, u32[]{:S(2)}) collective-permute-start(f32[344,128]{1,0:T(8,128)S(1)} %merge_two.1.refs_4_), channel_id=1, source_target_pairs={{0,4},{8,12},{1,5},{9,13},{2,6},{10,14},{3,7},{11,15},{16,20},{24,... | collective-permute-start | bytes 528392 | tf_op jit(solution)/shard_map/ppermute | solution.py:420
  14.6 1.1 %work.12 = (f32[640,128]{1,0:T(8,128)S(1)}, f32[640,128]{1,0:T(8,128)S(1)}) custom-call(bf16[640,2048]{1,0:T(8,128)(2,1)S(1)} %get-tuple-element.47.refs_0_, bf16[640,2048]{1,0:T(8,128)(2,1)S(1)} %get-tuple-element.48.k_ref.refs_1_, bf16[640,2048]{1,0:T(8,128)(2,1)S(1)} %get-tuple-element.49.v_ref.refs_2_, bf16[1,2048]{1,0:T(2,128)(2,1)S(1)} %reshape.3.refs_3_, ...), custom_call_target="tpu_custom_call" | custom-call | flops 1600001024 | bytes 1000 | tf_op jit(solution)/shard_map/work/pallas_call | solution.py:288
  15.6 0.0 collective-permute-done.8.received_ref.refs_7_.refs_4_
  15.7 0.7 %collective-permute-start.10 = (f32[344,128]{1,0:T(8,128)S(1)}, f32[344,128]{1,0:T(8,128)S(1)}, u32[]{:S(2)}, u32[]{:S(2)}) collective-permute-start(f32[344,128]{1,0:T(8,128)S(1)} %merge.14.order_ref), channel_id=1, source_target_pairs={{4,8},{5,9},{6,10},{7,11},{20,24},{21,25},{22,26},{23,27}} | collective-permute-start | bytes 528392 | tf_op jit(solution)/shard_map/ppermute | solution.py:392
  16.4 0.0 collective-permute-done.7.received_ref.refs_8_.refs_5_
  16.4 1.3 %collective-permute-start.9 = (f32[344,128]{1,0:T(8,128)S(1)}, f32[344,128]{1,0:T(8,128)S(1)}, u32[]{:S(2)}, u32[]{:S(2)}) collective-permute-start(f32[344,128]{1,0:T(8,128)S(1)} %merge.15.refs_4_), channel_id=1, source_target_pairs={{8,12},{9,13},{10,14},{11,15},{24,28},{25,29},{26,30},{27,31}} | collective-permute-start | bytes 528392 | tf_op jit(solution)/shard_map/ppermute | solution.py:392
  17.7 1.1 %work.13 = (f32[640,128]{1,0:T(8,128)S(1)}, f32[640,128]{1,0:T(8,128)S(1)}) custom-call(bf16[640,2048]{1,0:T(8,128)(2,1)S(1)} %get-tuple-element.47.refs_0_, bf16[640,2048]{1,0:T(8,128)(2,1)S(1)} %get-tuple-element.48.k_ref.refs_1_, bf16[640,2048]{1,0:T(8,128)(2,1)S(1)} %get-tuple-element.49.v_ref.refs_2_, bf16[1,2048]{1,0:T(2,128)(2,1)S(1)} %reshape.3.refs_3_, ...), custom_call_target="tpu_custom_call" | custom-call | flops 1600001024 | bytes 1000 | tf_op jit(solution)/shard_map/work/pallas_call | solution.py:288
  18.8 0.0 collective-permute-done.6.received_ref.refs_7_.refs_4_
  18.8 0.7 %collective-permute-start.12 = (f32[344,128]{1,0:T(8,128)S(1)}, f32[344,128]{1,0:T(8,128)S(1)}, u32[]{:S(2)}, u32[]{:S(2)}) collective-permute-start(f32[344,128]{1,0:T(8,128)S(1)} %merge.16.order_ref), channel_id=1, source_target_pairs={{4,8},{5,9},{6,10},{7,11},{20,24},{21,25},{22,26},{23,27}} | collective-permute-start | bytes 528392 | tf_op jit(solution)/shard_map/ppermute | solution.py:392
  19.5 0.0 collective-permute-done.5.received_ref.refs_8_.refs_5_
  19.5 1.3 %collective-permute-start.11 = (f32[344,128]{1,0:T(8,128)S(1)}, f32[344,128]{1,0:T(8,128)S(1)}, u32[]{:S(2)}, u32[]{:S(2)}) collective-permute-start(f32[344,128]{1,0:T(8,128)S(1)} %merge.17.refs_9_), channel_id=1, source_target_pairs={{8,12},{9,13},{10,14},{11,15},{24,28},{25,29},{26,30},{27,31}} | collective-permute-start | bytes 528392 | tf_op jit(solution)/shard_map/ppermute | solution.py:392
  20.8 1.0 %collective-permute-done.4.refs_6_.received_ref.refs_7_ = f32[344,128]{1,0:T(8,128)S(1)} collective-permute-done((f32[344,128]{1,0:T(8,128)S(1)}, f32[344,128]{1,0:T(8,128)S(1)}, u32[]{:S(2)}, u32[]{:S(2)}) %collective-permute-start.4) | collective-permute-done | bytes 176160 | tf_op jit(solution)/shard_map/ppermute | solution.py:420
  21.8 0.2 work.14
  22.1 0.7 %collective-permute-start.14 = (f32[344,128]{1,0:T(8,128)S(1)}, f32[344,128]{1,0:T(8,128)S(1)}, u32[]{:S(2)}, u32[]{:S(2)}) collective-permute-start(f32[344,128]{1,0:T(8,128)S(1)} %merge.18.order_ref), channel_id=1, source_target_pairs={{4,8},{5,9},{6,10},{7,11},{20,24},{21,25},{22,26},{23,27}} | collective-permute-start | bytes 528392 | tf_op jit(solution)/shard_map/ppermute | solution.py:392
  22.8 0.0 collective-permute-done.10.received_ref.refs_8_.refs_5_
  22.8 1.3 %collective-permute-start.13 = (f32[344,128]{1,0:T(8,128)S(1)}, f32[344,128]{1,0:T(8,128)S(1)}, u32[]{:S(2)}, u32[]{:S(2)}) collective-permute-start(f32[344,128]{1,0:T(8,128)S(1)} %merge.19.refs_14_), channel_id=1, source_target_pairs={{8,12},{9,13},{10,14},{11,15},{24,28},{25,29},{26,30},{27,31}} | collective-permute-start | bytes 528392 | tf_op jit(solution)/shard_map/ppermute | solution.py:392
  24.1 1.5 %collective-permute-done.9.refs_9_.refs_6_ = f32[344,128]{1,0:T(8,128)S(1)} collective-permute-done((f32[344,128]{1,0:T(8,128)S(1)}, f32[344,128]{1,0:T(8,128)S(1)}, u32[]{:S(2)}, u32[]{:S(2)}) %collective-permute-start.9) | collective-permute-done | bytes 176160 | tf_op jit(solution)/shard_map/ppermute | solution.py:392
  25.6 1.1 %work.15 = (f32[640,128]{1,0:T(8,128)S(1)}, f32[640,128]{1,0:T(8,128)S(1)}, f32[640,128]{1,0:T(8,128)S(1)}, f32[640,128]{1,0:T(8,128)S(1)}, f32[640,128]{1,0:T(8,128)S(1)}, /*index=5*/f32[640,128]{1,0:T(8,128)S(1)}) custom-call(bf16[640,2048]{1,0:T(8,128)(2,1)S(1)} %get-tuple-element.47.refs_0_, bf16[640,2048]{1,0:T(8,128)(2,1)S(1)} %get-tuple-element.48.k_ref.refs_1_, ...), custom_call_target="tpu_custom_call" | custom-call | flops 2200001024 | bytes 1000 | tf_op jit(solution)/shard_map/work/pallas_call | solution.py:288
  26.7 0.0 collective-permute-done.12.received_ref.refs_8_.refs_5_
  26.8 1.3 %collective-permute-start.15 = (f32[344,128]{1,0:T(8,128)S(1)}, f32[344,128]{1,0:T(8,128)S(1)}, u32[]{:S(2)}, u32[]{:S(2)}) collective-permute-start(f32[344,128]{1,0:T(8,128)S(1)} %merge.20.refs_13_), channel_id=1, source_target_pairs={{8,12},{9,13},{10,14},{11,15},{24,28},{25,29},{26,30},{27,31}} | collective-permute-start | bytes 528392 | tf_op jit(solution)/shard_map/ppermute | solution.py:392
  28.1 1.9 %collective-permute-done.11.refs_9_.refs_6_ = f32[344,128]{1,0:T(8,128)S(1)} collective-permute-done((f32[344,128]{1,0:T(8,128)S(1)}, f32[344,128]{1,0:T(8,128)S(1)}, u32[]{:S(2)}, u32[]{:S(2)}) %collective-permute-start.11) | collective-permute-done | bytes 176160 | tf_op jit(solution)/shard_map/ppermute | solution.py:392
  30.0 1.1 %work.16 = (f32[640,128]{1,0:T(8,128)S(1)}, f32[640,128]{1,0:T(8,128)S(1)}, f32[640,128]{1,0:T(8,128)S(1)}, f32[640,128]{1,0:T(8,128)S(1)}, f32[640,128]{1,0:T(8,128)S(1)}) custom-call(bf16[640,2048]{1,0:T(8,128)(2,1)S(1)} %get-tuple-element.47.refs_0_, bf16[640,2048]{1,0:T(8,128)(2,1)S(1)} %get-tuple-element.48.k_ref.refs_1_, ...), custom_call_target="tpu_custom_call" | custom-call | flops 2000001024 | bytes 1000 | tf_op jit(solution)/shard_map/work/pallas_call | solution.py:288
  31.1 0.0 collective-permute-done.14.received_ref.refs_8_
  31.1 1.5 %collective-permute-start.16 = (f32[344,128]{1,0:T(8,128)S(1)}, f32[344,128]{1,0:T(8,128)S(1)}, u32[]{:S(2)}, u32[]{:S(2)}) collective-permute-start(f32[344,128]{1,0:T(8,128)S(1)} %merge.21.refs_14_), channel_id=1, source_target_pairs={{8,12},{9,13},{10,14},{11,15},{24,28},{25,29},{26,30},{27,31}} | collective-permute-start | bytes 528392 | tf_op jit(solution)/shard_map/ppermute | solution.py:392
  32.6 1.3 %collective-permute-done.13.refs_9_.refs_6_ = f32[344,128]{1,0:T(8,128)S(1)} collective-permute-done((f32[344,128]{1,0:T(8,128)S(1)}, f32[344,128]{1,0:T(8,128)S(1)}, u32[]{:S(2)}, u32[]{:S(2)}) %collective-permute-start.13) | collective-permute-done | bytes 176160 | tf_op jit(solution)/shard_map/ppermute | solution.py:392
  34.0 1.1 %work.17 = (f32[640,128]{1,0:T(8,128)S(1)}, f32[640,128]{1,0:T(8,128)S(1)}, f32[640,128]{1,0:T(8,128)S(1)}, f32[640,128]{1,0:T(8,128)S(1)}, f32[640,128]{1,0:T(8,128)S(1)}, /*index=5*/f32[640,128]{1,0:T(8,128)S(1)}) custom-call(bf16[640,2048]{1,0:T(8,128)(2,1)S(1)} %get-tuple-element.47.refs_0_, bf16[640,2048]{1,0:T(8,128)(2,1)S(1)} %get-tuple-element.48.k_ref.refs_1_, ...), custom_call_target="tpu_custom_call" | custom-call | flops 2200001024 | bytes 1000 | tf_op jit(solution)/shard_map/work/pallas_call | solution.py:288
  35.1 3.1 %collective-permute-done.15.refs_9_.refs_6_ = f32[344,128]{1,0:T(8,128)S(1)} collective-permute-done((f32[344,128]{1,0:T(8,128)S(1)}, f32[344,128]{1,0:T(8,128)S(1)}, u32[]{:S(2)}, u32[]{:S(2)}) %collective-permute-start.15) | collective-permute-done | bytes 176160 | tf_op jit(solution)/shard_map/ppermute | solution.py:392
  38.2 0.3 work.18
  38.6 2.1 %collective-permute-done.16.refs_9_ = f32[344,128]{1,0:T(8,128)S(1)} collective-permute-done((f32[344,128]{1,0:T(8,128)S(1)}, f32[344,128]{1,0:T(8,128)S(1)}, u32[]{:S(2)}, u32[]{:S(2)}) %collective-permute-start.16) | collective-permute-done | bytes 176160 | tf_op jit(solution)/shard_map/ppermute | solution.py:392
  40.7 0.4 work.19
  41.1 1.6 %collective-permute-start.18 = (f32[1,640]{1,0:T(1,128)S(1)}, f32[1,640]{1,0:T(1,128)S(1)}, u32[]{:S(2)}, u32[]{:S(2)}) collective-permute-start(f32[1,640]{1,0:T(1,128)S(1)} %get-tuple-element.88), channel_id=1, source_target_pairs={{0,2},{1,3},{2,0},{3,1},{4,6},{5,7},{6,4},{7,5},{8,10},{9,11},{10,... | collective-permute-start | bytes 7688 | tf_op jit(solution)/shard_map/ppermute | solution.py:358
  42.7 0.0 collective-permute-start.19
  42.7 0.6 %collective-permute-start.17 = (f32[1,640]{1,0:T(1,128)S(1)}, f32[1,640]{1,0:T(1,128)S(1)}, u32[]{:S(2)}, u32[]{:S(2)}) collective-permute-start(f32[1,640]{1,0:T(1,128)S(1)} %get-tuple-element.88), channel_id=1, source_target_pairs={{0,1},{1,0},{2,3},{3,2},{4,5},{5,4},{6,7},{7,6},{8,9},{9,8},{10,11... | collective-permute-start | bytes 7688 | tf_op jit(solution)/shard_map/ppermute | solution.py:358
  43.3 1.4 %collective-permute-done.18 = f32[1,640]{1,0:T(1,128)S(1)} collective-permute-done((f32[1,640]{1,0:T(1,128)S(1)}, f32[1,640]{1,0:T(1,128)S(1)}, u32[]{:S(2)}, u32[]{:S(2)}) %collective-permute-start.18) | collective-permute-done | bytes 2592 | tf_op jit(solution)/shard_map/ppermute | solution.py:358
  44.7 0.9 %collective-permute-done.19 = f32[1,640]{1,0:T(1,128)S(1)} collective-permute-done((f32[1,640]{1,0:T(1,128)S(1)}, f32[1,640]{1,0:T(1,128)S(1)}, u32[]{:S(2)}, u32[]{:S(2)}) %collective-permute-start.19) | collective-permute-done | bytes 2592 | tf_op jit(solution)/shard_map/ppermute | solution.py:358
  45.7 0.0 collective-permute-done.17
  45.7 1.7 %finish.1 = bf16[640,2048]{1,0:T(8,128)(2,1)} custom-call(f32[640,128]{1,0:T(8,128)S(1)} %get-tuple-element.57.refs_0_, f32[640,128]{1,0:T(8,128)S(1)} %get-tuple-element.58.refs_1_, f32[640,128]{1,0:T(8,128)S(1)} %get-tuple-element.62.refs_2_, f32[640,128]{1,0:T(8,128)S(1)} %get-tuple-element.63.refs_3_, f32[640,128]{1,0:T(8,128)S(1)} %get-tuple-element.64.refs_4_, ...), custom_call_target="tpu_custom_call" | custom-call | tf_op jit(solution)/shard_map/finish/pallas_call | solution.py:339
  (14 shorter events, 0.3 us)
Async XLA Ops:
  1.5 4.8 %collective-permute-start = (f32[328,128]{1,0:T(8,128)S(1)}, f32[328,128]{1,0:T(8,128)S(1)}, u32[]{:S(2)}, u32[]{:S(2)}) collective-permute-start(f32[328,128]{1,0:T(8,128)S(1)} %first.1.order_ref.state_ref), channel_id=1, source_target_pairs={{0,4},{1,5},{2,6},{3,7},{4,0},{5,1},{6,2},{7,3},{8,9},{9,8},{10,11... | collective-permute-start | bytes 503816 | tf_op jit(solution)/shard_map/ppermute | solution.py:390
  5.1 4.2 %collective-permute-start.3 = (f32[344,128]{1,0:T(8,128)S(1)}, f32[344,128]{1,0:T(8,128)S(1)}, u32[]{:S(2)}, u32[]{:S(2)}) collective-permute-start(f32[344,128]{1,0:T(8,128)S(1)} %get-tuple-element.50.order_ref.state_ref), channel_id=1, source_target_pairs={{0,4},{1,5},{2,6},{3,7},{4,0},{5,1},{6,2},{7,3},{8,9},{9,8},{10,11... | collective-permute-start | bytes 528392 | tf_op jit(solution)/shard_map/ppermute | solution.py:390
  5.6 0.7 %copy-start = (bf16[2048]{0:T(1024)(128)(2,1)S(1)}, bf16[2048]{0:T(1024)(128)(2,1)}, u32[]{:S(2)}) copy-start(bf16[2048]{0:T(1024)(128)(2,1)} %param.7) | copy-start | bytes 12292
  6.0 6.1 %collective-permute-start.2 = (f32[344,128]{1,0:T(8,128)S(1)}, f32[344,128]{1,0:T(8,128)S(1)}, u32[]{:S(2)}, u32[]{:S(2)}) collective-permute-start(f32[344,128]{1,0:T(8,128)S(1)} %states.4.order_ref.state_ref), channel_id=1, source_target_pairs={{0,4},{1,5},{2,6},{3,7},{4,0},{5,1},{6,2},{7,3},{8,9},{9,8},{10,11... | collective-permute-start | bytes 528392 | tf_op jit(solution)/shard_map/ppermute | solution.py:390
  6.4 6.9 %collective-permute-start.1 = (f32[328,128]{1,0:T(8,128)S(1)}, f32[328,128]{1,0:T(8,128)S(1)}, u32[]{:S(2)}, u32[]{:S(2)}) collective-permute-start(f32[328,128]{1,0:T(8,128)S(1)} %merge.11.order_ref), channel_id=1, source_target_pairs={{4,8},{5,9},{6,10},{7,11},{20,24},{21,25},{22,26},{23,27}} | collective-permute-start | bytes 503816 | tf_op jit(solution)/shard_map/ppermute | solution.py:392
  7.5 8.2 %collective-permute-start.8 = (f32[344,128]{1,0:T(8,128)S(1)}, f32[344,128]{1,0:T(8,128)S(1)}, u32[]{:S(2)}, u32[]{:S(2)}) collective-permute-start(f32[344,128]{1,0:T(8,128)S(1)} %states.5.refs_4_.state_ref), channel_id=1, source_target_pairs={{0,4},{1,5},{2,6},{3,7},{4,0},{5,1},{6,2},{7,3},{8,9},{9,8},{10,11... | collective-permute-start | bytes 528392 | tf_op jit(solution)/shard_map/ppermute | solution.py:390
  9.7 6.7 %collective-permute-start.7 = (f32[344,128]{1,0:T(8,128)S(1)}, f32[344,128]{1,0:T(8,128)S(1)}, u32[]{:S(2)}, u32[]{:S(2)}) collective-permute-start(f32[344,128]{1,0:T(8,128)S(1)} %merge.12.order_ref), channel_id=1, source_target_pairs={{4,8},{5,9},{6,10},{7,11},{20,24},{21,25},{22,26},{23,27}} | collective-permute-start | bytes 528392 | tf_op jit(solution)/shard_map/ppermute | solution.py:392
  11.8 6.9 %collective-permute-start.6 = (f32[344,128]{1,0:T(8,128)S(1)}, f32[344,128]{1,0:T(8,128)S(1)}, u32[]{:S(2)}, u32[]{:S(2)}) collective-permute-start(f32[344,128]{1,0:T(8,128)S(1)} %states.6.refs_4_.state_ref), channel_id=1, source_target_pairs={{0,4},{1,5},{2,6},{3,7},{4,0},{5,1},{6,2},{7,3},{8,9},{9,8},{10,11... | collective-permute-start | bytes 528392 | tf_op jit(solution)/shard_map/ppermute | solution.py:390
  12.2 7.3 %collective-permute-start.5 = (f32[344,128]{1,0:T(8,128)S(1)}, f32[344,128]{1,0:T(8,128)S(1)}, u32[]{:S(2)}, u32[]{:S(2)}) collective-permute-start(f32[344,128]{1,0:T(8,128)S(1)} %merge.13.order_ref), channel_id=1, source_target_pairs={{4,8},{5,9},{6,10},{7,11},{20,24},{21,25},{22,26},{23,27}} | collective-permute-start | bytes 528392 | tf_op jit(solution)/shard_map/ppermute | solution.py:392
  13.3 8.5 %collective-permute-start.4 = (f32[344,128]{1,0:T(8,128)S(1)}, f32[344,128]{1,0:T(8,128)S(1)}, u32[]{:S(2)}, u32[]{:S(2)}) collective-permute-start(f32[344,128]{1,0:T(8,128)S(1)} %merge_two.1.refs_4_), channel_id=1, source_target_pairs={{0,4},{8,12},{1,5},{9,13},{2,6},{10,14},{3,7},{11,15},{16,20},{24,... | collective-permute-start | bytes 528392 | tf_op jit(solution)/shard_map/ppermute | solution.py:420
  15.7 7.1 %collective-permute-start.10 = (f32[344,128]{1,0:T(8,128)S(1)}, f32[344,128]{1,0:T(8,128)S(1)}, u32[]{:S(2)}, u32[]{:S(2)}) collective-permute-start(f32[344,128]{1,0:T(8,128)S(1)} %merge.14.order_ref), channel_id=1, source_target_pairs={{4,8},{5,9},{6,10},{7,11},{20,24},{21,25},{22,26},{23,27}} | collective-permute-start | bytes 528392 | tf_op jit(solution)/shard_map/ppermute | solution.py:392
  16.4 9.2 %collective-permute-start.9 = (f32[344,128]{1,0:T(8,128)S(1)}, f32[344,128]{1,0:T(8,128)S(1)}, u32[]{:S(2)}, u32[]{:S(2)}) collective-permute-start(f32[344,128]{1,0:T(8,128)S(1)} %merge.15.refs_4_), channel_id=1, source_target_pairs={{8,12},{9,13},{10,14},{11,15},{24,28},{25,29},{26,30},{27,31}} | collective-permute-start | bytes 528392 | tf_op jit(solution)/shard_map/ppermute | solution.py:392
  18.8 7.9 %collective-permute-start.12 = (f32[344,128]{1,0:T(8,128)S(1)}, f32[344,128]{1,0:T(8,128)S(1)}, u32[]{:S(2)}, u32[]{:S(2)}) collective-permute-start(f32[344,128]{1,0:T(8,128)S(1)} %merge.16.order_ref), channel_id=1, source_target_pairs={{4,8},{5,9},{6,10},{7,11},{20,24},{21,25},{22,26},{23,27}} | collective-permute-start | bytes 528392 | tf_op jit(solution)/shard_map/ppermute | solution.py:392
  19.5 10.4 %collective-permute-start.11 = (f32[344,128]{1,0:T(8,128)S(1)}, f32[344,128]{1,0:T(8,128)S(1)}, u32[]{:S(2)}, u32[]{:S(2)}) collective-permute-start(f32[344,128]{1,0:T(8,128)S(1)} %merge.17.refs_9_), channel_id=1, source_target_pairs={{8,12},{9,13},{10,14},{11,15},{24,28},{25,29},{26,30},{27,31}} | collective-permute-start | bytes 528392 | tf_op jit(solution)/shard_map/ppermute | solution.py:392
  22.1 9.0 %collective-permute-start.14 = (f32[344,128]{1,0:T(8,128)S(1)}, f32[344,128]{1,0:T(8,128)S(1)}, u32[]{:S(2)}, u32[]{:S(2)}) collective-permute-start(f32[344,128]{1,0:T(8,128)S(1)} %merge.18.order_ref), channel_id=1, source_target_pairs={{4,8},{5,9},{6,10},{7,11},{20,24},{21,25},{22,26},{23,27}} | collective-permute-start | bytes 528392 | tf_op jit(solution)/shard_map/ppermute | solution.py:392
  22.8 11.1 %collective-permute-start.13 = (f32[344,128]{1,0:T(8,128)S(1)}, f32[344,128]{1,0:T(8,128)S(1)}, u32[]{:S(2)}, u32[]{:S(2)}) collective-permute-start(f32[344,128]{1,0:T(8,128)S(1)} %merge.19.refs_14_), channel_id=1, source_target_pairs={{8,12},{9,13},{10,14},{11,15},{24,28},{25,29},{26,30},{27,31}} | collective-permute-start | bytes 528392 | tf_op jit(solution)/shard_map/ppermute | solution.py:392
  26.8 11.5 %collective-permute-start.15 = (f32[344,128]{1,0:T(8,128)S(1)}, f32[344,128]{1,0:T(8,128)S(1)}, u32[]{:S(2)}, u32[]{:S(2)}) collective-permute-start(f32[344,128]{1,0:T(8,128)S(1)} %merge.20.refs_13_), channel_id=1, source_target_pairs={{8,12},{9,13},{10,14},{11,15},{24,28},{25,29},{26,30},{27,31}} | collective-permute-start | bytes 528392 | tf_op jit(solution)/shard_map/ppermute | solution.py:392
  31.1 9.5 %collective-permute-start.16 = (f32[344,128]{1,0:T(8,128)S(1)}, f32[344,128]{1,0:T(8,128)S(1)}, u32[]{:S(2)}, u32[]{:S(2)}) collective-permute-start(f32[344,128]{1,0:T(8,128)S(1)} %merge.21.refs_14_), channel_id=1, source_target_pairs={{8,12},{9,13},{10,14},{11,15},{24,28},{25,29},{26,30},{27,31}} | collective-permute-start | bytes 528392 | tf_op jit(solution)/shard_map/ppermute | solution.py:392
  41.1 3.7 %collective-permute-start.18 = (f32[1,640]{1,0:T(1,128)S(1)}, f32[1,640]{1,0:T(1,128)S(1)}, u32[]{:S(2)}, u32[]{:S(2)}) collective-permute-start(f32[1,640]{1,0:T(1,128)S(1)} %get-tuple-element.88), channel_id=1, source_target_pairs={{0,2},{1,3},{2,0},{3,1},{4,6},{5,7},{6,4},{7,5},{8,10},{9,11},{10,... | collective-permute-start | bytes 7688 | tf_op jit(solution)/shard_map/ppermute | solution.py:358
  42.7 3.0 %collective-permute-start.19 = (f32[1,640]{1,0:T(1,128)S(1)}, f32[1,640]{1,0:T(1,128)S(1)}, u32[]{:S(2)}, u32[]{:S(2)}) collective-permute-start(f32[1,640]{1,0:T(1,128)S(1)} %get-tuple-element.88), channel_id=1, source_target_pairs={{0,3},{1,2},{2,1},{3,0},{4,7},{5,6},{6,5},{7,4},{8,11},{9,10},{10,... | collective-permute-start | bytes 7688 | tf_op jit(solution)/shard_map/ppermute | solution.py:358
  42.7 3.0 %collective-permute-start.17 = (f32[1,640]{1,0:T(1,128)S(1)}, f32[1,640]{1,0:T(1,128)S(1)}, u32[]{:S(2)}, u32[]{:S(2)}) collective-permute-start(f32[1,640]{1,0:T(1,128)S(1)} %get-tuple-element.88), channel_id=1, source_target_pairs={{0,1},{1,0},{2,3},{3,2},{4,5},{5,4},{6,7},{7,6},{8,9},{9,8},{10,11... | collective-permute-start | bytes 7688 | tf_op jit(solution)/shard_map/ppermute | solution.py:358
